TPU v7x, 512 devices: a whole 4x4x16 slice. The times are simulated.
512 devices in a mesh: ctx: 64 (over x_lo, z, core), ch: 8 (over y, x_hi).
Axes of the slice: x: 4 (x_hi: 2, x_lo: 2; x = x_hi * 2 + x_lo), y: 4, z: 16, core: 2. Of those that a mesh axis runs over, the one named last changes fastest.
Arguments:
- streams: bfloat16 [3, 8192, 2048], P(None, 'ctx', 'ch'), may hold values from -6 to 6
- short_weight: float32 [3, 3, 2048], P(None, None, 'ch'), may hold values from -3 to 3
- filt_first: bfloat16 [2, 5, 64], replicated, may hold values from -2.5 to 2.5
- filt_bias: float32 [2, 2, 64], replicated, may hold values from -4 to 4
- filt_mid: bfloat16 [2, 64, 64], replicated, may hold values from -0.75 to 0.75
- filt_freq: float32 [2, 64], replicated, may hold values from 0.5 to 2
- filt_last: bfloat16 [2, 64, 2048], P(None, None, 'ch'), may hold values from -0.75 to 0.75
- decay: float32 [2, 2048], P(None, 'ch'), may hold values from 3.0517578e-05 to 0.03
- skip: float32 [2, 2048], P(None, 'ch'), may hold values from -4 to 4
- out_weight: bfloat16 [2048, 4096], P('ch'), may hold values from -0.125 to 0.125
Outputs:
- mixed: bfloat16 [8192, 4096], P('ctx', 'ch')
All inputs are finite; a program needn't handle non-finite values.
Results may differ from a plain program's by a relative error of at most 0.01.
The roundings to bfloat16 on the way count: a program that leaves them out, or rounds other values in their place, can miss the bound.
Values may be sent and summed in bfloat16 or wider, within the bound.
A program may use at most 64 MiB of HBM per device.

v0:
```python
import math

import jax
import jax.numpy as jnp
from jax import lax
from jax.sharding import PartitionSpec as P

EMB = 5


def shifted(x, axis, by):
    count = lax.axis_size(axis)
    pairs = [(i, i + by) for i in range(count) if 0 <= i + by < count]
    return lax.ppermute(x, axis, pairs)


def features(positions, seq_len):
    bands = (EMB - 1) // 2
    cols = [positions.astype(jnp.float32) / seq_len]
    cosines = []
    sines = []
    for band in range(bands):
        wrapped = (band + 1) * positions % seq_len
        angle = 2.0 * math.pi / seq_len * wrapped.astype(jnp.float32)
        cosines.append(jnp.cos(angle))
        sines.append(jnp.sin(angle))
    return jnp.stack(cols + cosines + sines, axis=-1)


def hidden_rows(positions, seq_len, first, bias, mid, freq):
    feat = features(positions, seq_len).astype(jnp.bfloat16)
    act_one = jnp.sin(
        freq * (jnp.dot(feat, first, preferred_element_type=jnp.float32) + bias[0])
    ).astype(jnp.bfloat16)
    return jnp.sin(
        freq * (jnp.dot(act_one, mid, preferred_element_type=jnp.float32) + bias[1])
    ).astype(jnp.bfloat16)


def filter_columns(positions, seq_len, first, bias, mid, freq, last, rate):
    act_two = hidden_rows(positions, seq_len, first, bias, mid, freq)
    raw = jnp.einsum("kc,pk->cp", last, act_two, preferred_element_type=jnp.float32)
    lagged = positions.astype(jnp.float32)[None, :]
    return raw * jnp.exp(-rate[:, None] * lagged) * jnp.sqrt(2.0 * rate)[:, None]


def window_tables(total_len):
    panel = 128
    rows_a = total_len // panel
    half = rows_a // 2
    freq_a = jnp.arange(rows_a, dtype=jnp.int32)[:, None]
    sample_a = jnp.arange(half, dtype=jnp.int32)[None, :]
    angle_a = 2.0 * math.pi / rows_a * (freq_a * sample_a % rows_a).astype(jnp.float32)
    fwd_a = (jnp.cos(angle_a), -jnp.sin(angle_a))
    back_a = (jnp.cos(angle_a).T / total_len, jnp.sin(angle_a).T / total_len)
    cols_b = jnp.arange(panel, dtype=jnp.int32)[None, :]
    angle_t = 2.0 * math.pi / total_len * (freq_a * cols_b % total_len).astype(jnp.float32)
    twiddle = (jnp.cos(angle_t), -jnp.sin(angle_t))
    rows_b = jnp.arange(panel, dtype=jnp.int32)[:, None]
    angle_b = 2.0 * math.pi / panel * (rows_b * cols_b % panel).astype(jnp.float32)
    fwd_b = (jnp.cos(angle_b), -jnp.sin(angle_b))
    back_b = (jnp.cos(angle_b), jnp.sin(angle_b))
    return (fwd_a, back_a, twiddle, fwd_b, back_b)


def window_forward(values, tables):
    fwd_a, back_a, twiddle, fwd_b, back_b = tables
    highest = lax.Precision.HIGHEST
    step_re = jnp.einsum("ka,cab->ckb", fwd_a[0], values, precision=highest)
    step_im = jnp.einsum("ka,cab->ckb", fwd_a[1], values, precision=highest)
    turn_re = step_re * twiddle[0] - step_im * twiddle[1]
    turn_im = step_re * twiddle[1] + step_im * twiddle[0]
    spec_re = jnp.einsum("ckb,bj->ckj", turn_re, fwd_b[0], precision=highest) - jnp.einsum(
        "ckb,bj->ckj", turn_im, fwd_b[1], precision=highest
    )
    spec_im = jnp.einsum("ckb,bj->ckj", turn_re, fwd_b[1], precision=highest) + jnp.einsum(
        "ckb,bj->ckj", turn_im, fwd_b[0], precision=highest
    )
    return (spec_re, spec_im)


def window_inverse(spec_re, spec_im, tables):
    fwd_a, back_a, twiddle, fwd_b, back_b = tables
    highest = lax.Precision.HIGHEST
    step_re = jnp.einsum("ckj,jb->ckb", spec_re, back_b[0], precision=highest) - jnp.einsum(
        "ckj,jb->ckb", spec_im, back_b[1], precision=highest
    )
    step_im = jnp.einsum("ckj,jb->ckb", spec_re, back_b[1], precision=highest) + jnp.einsum(
        "ckj,jb->ckb", spec_im, back_b[0], precision=highest
    )
    turn_re = step_re * twiddle[0] + step_im * twiddle[1]
    turn_im = step_im * twiddle[0] - step_re * twiddle[1]
    return jnp.einsum("ak,ckb->cab", back_a[0], turn_re, precision=highest) - jnp.einsum(
        "ak,ckb->cab", back_a[1], turn_im, precision=highest
    )


def channel_conv(state_cols, order, params, tables, seq_len):
    filt_first, filt_bias, filt_mid, filt_freq, filt_last, decay = params
    per_group = state_cols.shape[0] // lax.axis_size("ctx")
    gathered = lax.all_to_all(state_cols, "ctx", split_axis=0, concat_axis=1, tiled=True)
    offset = lax.axis_index("ctx") * per_group
    last = lax.dynamic_slice_in_dim(filt_last[order], offset, per_group, 1)
    rate = lax.dynamic_slice_in_dim(decay[order], offset, per_group, 0)
    positions = jnp.arange(seq_len, dtype=jnp.int32)
    filt = filter_columns(
        positions,
        seq_len,
        filt_first[order],
        filt_bias[order],
        filt_mid[order],
        filt_freq[order],
        last,
        rate,
    )
    half = seq_len // 128
    signal = gathered.astype(jnp.float32).reshape(per_group, half, 128)
    sig_re, sig_im = window_forward(signal, tables)
    filt_re, filt_im = window_forward(filt.reshape(per_group, half, 128), tables)
    prod_re = filt_re * sig_re - filt_im * sig_im
    prod_im = filt_re * sig_im + filt_im * sig_re
    conv = window_inverse(prod_re, prod_im, tables).reshape(per_group, seq_len)
    return lax.all_to_all(conv, "ctx", split_axis=1, concat_axis=0, tiled=True)


def per_device(
    streams,
    short_weight,
    filt_first,
    filt_bias,
    filt_mid,
    filt_freq,
    filt_last,
    decay,
    skip,
    out_weight,
):
    tok = streams.shape[1]
    seq_len = tok * lax.axis_size("ctx")
    before = shifted(streams[:, tok - 2 :, :], "ctx", 1)
    joined = jnp.concatenate([before, streams], axis=1).astype(jnp.float32)
    shortened = (
        short_weight[:, 0][:, None, :] * joined[:, 2:]
        + short_weight[:, 1][:, None, :] * joined[:, 1:-1]
        + short_weight[:, 2][:, None, :] * joined[:, :-2]
    ).astype(jnp.bfloat16)
    params = (filt_first, filt_bias, filt_mid, filt_freq, filt_last, decay)
    tables = window_tables(2 * seq_len)
    shortened_cols = jnp.swapaxes(shortened, 1, 2)
    state = shortened_cols[0]
    for order in range(2):
        conv = channel_conv(state, order, params, tables, seq_len)
        output = conv + skip[order][:, None] * state.astype(jnp.float32)
        state = (shortened_cols[order + 1].astype(jnp.float32) * output).astype(jnp.bfloat16)
    contract = 0
    share = lax.psum_scatter(
        lax.dot_general(
            out_weight, state, (((0,), (contract,)), ((), ())), preferred_element_type=jnp.float32
        ),
        "ch",
        scatter_dimension=0,
        tiled=True,
    )
    return share.T.astype(jnp.bfloat16)


def solution(mesh):
    return jax.shard_map(
        per_device,
        mesh=mesh,
        in_specs=(
            P(None, "ctx", "ch"),
            P(None, None, "ch"),
            P(),
            P(),
            P(),
            P(),
            P(None, None, "ch"),
            P(None, "ch"),
            P(None, "ch"),
            P("ch", None),
        ),
        out_specs=P("ctx", "ch"),
        check_vma=False,
    )
```

profile of v0, /device:TPU:1, one launch (start us, length us, event | category | flops | bytes accessed | tf_op | source)
XLA Modules:
  0.0 269.8 jit_solution(15998991697433477936)
XLA Ops:
  6.5 0.9 slice.89
  7.4 0.8 copy.82
  8.2 4.9 %collective-permute-start = (bf16[3,2,256]{1,2,0:T(8,128)(2,1)}, bf16[3,2,256]{1,2,0:T(8,128)(2,1)}, u32[]{:S(2)}, u32[]{:S(2)}) collective-permute-start(bf16[3,2,256]{1,2,0:T(8,128)(2,1)} %copy.82), channel_id=1, source_target_pairs={{0,8},{8,16},{16,24},{24,32},{32,40},{40,48},{48,56},{56,64},{64,7... | collective-permute-start | bytes 9224 | tf_op jit(solution)/shard_map/ppermute | solution.py:14
  13.8 1.9 cosine_convert_fusion
  15.7 2.1 sine_convert_fusion
  19.3 0.8 fusion.367
  20.1 0.8 fusion.365
  20.9 0.8 fusion.363
  22.0 16.5 %fusion.10 = bf16[8192,64]{0,1:T(8,128)(2,1)} fusion(bf16[8192,5]{0,1:T(8,128)(2,1)S(1)} %stack.3, f32[64]{0:T(128)S(1)} %get-tuple-element.26, f32[64]{0:T(128)S(1)} %get-tuple-element.23, f32[64]{0:T(128)S(1)} %get-tuple-element.29, bf16[2,64,64]{2,1,0:T(8,128)(2,1)} %param.14, bf16[1,5,64]{2,0,1:T(2,128)(2,1)S(1)} %get-tuple-element.16), kind=kOutput, calls=%fused_computation.14 | convolution fusion | flops 75497472 | bytes 1200640 | tf_op jit(solution)/shard_map/dot_general | solution.py:36
  38.5 1.6 fusion.15
  42.4 1.4 fusion.105
  43.8 15.6 %fusion.11 = bf16[8192,64]{0,1:T(8,128)(2,1)} fusion(bf16[8192,5]{0,1:T(8,128)(2,1)S(1)} %stack.3, f32[64]{0:T(128)S(1)} %get-tuple-element.24, f32[64]{0:T(128)S(1)} %get-tuple-element.25, f32[64]{0:T(128)S(1)} %get-tuple-element.30, bf16[2,64,64]{2,1,0:T(8,128)(2,1)S(1)} %copy-done.6, bf16[1,5,64]{2,0,1:T(2,128)(2,1)S(1)} %get-tuple-element.17), kind=kOutput, calls=%fused_computation.15 | convolution fusion | flops 75497472 | bytes 1200640 | tf_op jit(solution)/shard_map/dot_general | solution.py:36
  59.4 1.6 fusion.14
  61.0 1.1 copy.83
  62.1 1.1 maximum_convert_fusion
  64.6 16.1 %all-to-all-start = ((bf16[64,4,128]{2,1,0:T(4,128)(2,1)}), bf16[64,4,128]{2,1,0:T(4,128)(2,1)S(1)}, u32[]{:S(2)}, u32[]{:S(2)}) async-start(bf16[64,4,128]{2,1,0:T(4,128)(2,1)} %bitcast.27), calls=%async_computation | async-start | bytes 131072 | tf_op jit(solution)/shard_map/all_to_all | solution.py:101
  81.3 2.4 convolution_subtract_fusion.4
  83.7 11.5 %all-to-all-done = bf16[64,4,128]{2,1,0:T(4,128)(2,1)S(1)} async-done(((bf16[64,4,128]{2,1,0:T(4,128)(2,1)}), bf16[64,4,128]{2,1,0:T(4,128)(2,1)S(1)}, u32[]{:S(2)}, u32[]{:S(2)}) %all-to-all-start) | async-done | bytes 65568 | tf_op jit(solution)/shard_map/all_to_all | solution.py:101
  96.1 0.8 fusion.84
  98.4 0.8 convolution_subtract_fusion.3
  99.2 0.8 multiply_add_fusion.2
  104.4 4.4 %all-to-all-start.1 = ((f32[4,64,128]{2,0,1:T(4,128)}), f32[4,64,128]{2,0,1:T(4,128)S(1)}, u32[]{:S(2)}, u32[]{:S(2)}) async-start(f32[4,64,128]{2,0,1:T(4,128)} %copy.105), calls=%async_computation.1 | async-start | bytes 262144 | tf_op jit(solution)/shard_map/all_to_all | solution.py:123
  110.4 15.7 %all-to-all-done.1 = f32[4,64,128]{2,0,1:T(4,128)S(1)} async-done(((f32[4,64,128]{2,0,1:T(4,128)}), f32[4,64,128]{2,0,1:T(4,128)S(1)}, u32[]{:S(2)}, u32[]{:S(2)}) %all-to-all-start.1) | async-done | bytes 131104 | tf_op jit(solution)/shard_map/all_to_all | solution.py:123
  126.1 1.6 fusion.49
  127.7 4.7 %all-to-all-start.2 = ((bf16[64,4,128]{2,1,0:T(4,128)(2,1)}), bf16[64,4,128]{2,1,0:T(4,128)(2,1)S(1)}, u32[]{:S(2)}, u32[]{:S(2)}) async-start(bf16[64,4,128]{2,1,0:T(4,128)(2,1)} %fusion.49), calls=%async_computation.2 | async-start | bytes 131072 | tf_op jit(solution)/shard_map/all_to_all | solution.py:101
  134.0 13.1 %all-to-all-done.2 = bf16[64,4,128]{2,1,0:T(4,128)(2,1)S(1)} async-done(((bf16[64,4,128]{2,1,0:T(4,128)(2,1)}), bf16[64,4,128]{2,1,0:T(4,128)(2,1)S(1)}, u32[]{:S(2)}, u32[]{:S(2)}) %all-to-all-start.2) | async-done | bytes 65568 | tf_op jit(solution)/shard_map/all_to_all | solution.py:101
  147.9 0.8 fusion.79
  150.2 0.8 convolution_subtract_fusion.1
  155.6 20.8 %all_to_all.61 = f32[4,64,128]{2,0,1:T(4,128)S(1)} all-to-all(f32[4,64,128]{2,0,1:T(4,128)S(1)} %copy.119), channel_id=1, replica_groups=mesh['ctx'=64,'ch'=8] {'ctx'}, dimensions={1} | all-to-all | bytes 262144 | tf_op jit(solution)/shard_map/all_to_all | solution.py:123
  176.4 2.8 %convolution_bitcast_fusion = f32[4096,128]{0,1:T(8,128)} fusion(bf16[256,4096]{1,0:T(8,128)(2,1)S(1)} %copy-done, f32[256,128]{1,0:T(8,128)S(1)} %bitcast.226, f32[256,128]{1,0:T(8,128)S(1)} %bitcast.225, bf16[3,256,128]{2,1,0:T(8,128)(2,1)} %copy-done.2, f32[256]{0:T(256)S(1)} %bitcast.230, f32[256]{0:T(256)S(1)} %bitcast.229), kind=kOutput, calls=%fused_computation.20 | convolution fusion | flops 268828672 | bytes 4655104 | tf_op jit(solution)/shard_map/dot_general | solution.py:157
  179.2 81.6 %reduce-scatter.2.cloned.1.call-done = f32[512,128]{0,1:T(8,128)} async-done(((f32[4096,128]{0,1:T(8,128)}), f32[512,128]{0,1:T(8,128)}) %reduce-scatter.2.cloned.1.call-update) | async-done | bytes 262160 | tf_op jit(solution)/shard_map/reduce_scatter | solution.py:156
  260.8 1.6 convert_bitcast_fusion
  (65 shorter events, 23.3 us)
Async XLA Ops:
  6.5 169.9 %copy-start = (bf16[256,4096]{1,0:T(8,128)(2,1)S(1)}, bf16[256,4096]{1,0:T(8,128)(2,1)}, u32[]{:S(2)}) copy-start(bf16[256,4096]{1,0:T(8,128)(2,1)} %param.19) | copy-start | bytes 6291460
  8.2 53.9 %collective-permute-start = (bf16[3,2,256]{1,2,0:T(8,128)(2,1)}, bf16[3,2,256]{1,2,0:T(8,128)(2,1)}, u32[]{:S(2)}, u32[]{:S(2)}) collective-permute-start(bf16[3,2,256]{1,2,0:T(8,128)(2,1)} %copy.82), channel_id=1, source_target_pairs={{0,8},{8,16},{16,24},{24,32},{32,40},{40,48},{48,56},{56,64},{64,7... | collective-permute-start | bytes 9224 | tf_op jit(solution)/shard_map/ppermute | solution.py:14
  38.5 5.3 %copy-start.4 = (f32[3,3,256]{2,1,0:T(4,128)S(1)}, f32[3,3,256]{2,1,0:T(4,128)}, u32[]{:S(2)}) copy-start(f32[3,3,256]{2,1,0:T(4,128)} %param.11) | copy-start | bytes 27652
  38.5 5.3 %copy-start.6 = (bf16[2,64,64]{2,1,0:T(8,128)(2,1)S(1)}, bf16[2,64,64]{2,1,0:T(8,128)(2,1)}, u32[]{:S(2)}) copy-start(bf16[2,64,64]{2,1,0:T(8,128)(2,1)} %param.14) | copy-start | bytes 49156
  63.8 0.8 copy-start.2
  64.6 30.7 %all-to-all-start = ((bf16[64,4,128]{2,1,0:T(4,128)(2,1)}), bf16[64,4,128]{2,1,0:T(4,128)(2,1)S(1)}, u32[]{:S(2)}, u32[]{:S(2)}) async-start(bf16[64,4,128]{2,1,0:T(4,128)(2,1)} %bitcast.27), calls=%async_computation | async-start | bytes 131072 | tf_op jit(solution)/shard_map/all_to_all | solution.py:101
  96.1 3.1 %copy-start.1 = (f32[4,128,128]{2,1,0:T(8,128)S(1)}, f32[4,128,128]{2,1,0:T(8,128)}, u32[]{:S(2)}) copy-start(f32[4,128,128]{2,1,0:T(8,128)} %convolution_subtract_fusion.4) | copy-start | bytes 786436
  100.6 8.3 %copy-start.5 = (f32[2,256]{1,0:T(2,128)S(1)}, f32[2,256]{1,0:T(2,128)}, u32[]{:S(2)}) copy-start(f32[2,256]{1,0:T(2,128)} %param.18) | copy-start | bytes 6148
  101.9 24.2 %copy-start.3 = (f32[1,256,128]{2,1,0:T(8,128)S(1)}, f32[1,256,128]{2,1,0:T(8,128)}, u32[]{:S(2)}) copy-start(f32[1,256,128]{2,1,0:T(8,128)} %get-tuple-element.10) | copy-start | bytes 393220
  104.4 21.7 %all-to-all-start.1 = ((f32[4,64,128]{2,0,1:T(4,128)}), f32[4,64,128]{2,0,1:T(4,128)S(1)}, u32[]{:S(2)}, u32[]{:S(2)}) async-start(f32[4,64,128]{2,0,1:T(4,128)} %copy.105), calls=%async_computation.1 | async-start | bytes 262144 | tf_op jit(solution)/shard_map/all_to_all | solution.py:123
  127.7 19.4 %all-to-all-start.2 = ((bf16[64,4,128]{2,1,0:T(4,128)(2,1)}), bf16[64,4,128]{2,1,0:T(4,128)(2,1)S(1)}, u32[]{:S(2)}, u32[]{:S(2)}) async-start(bf16[64,4,128]{2,1,0:T(4,128)(2,1)} %fusion.49), calls=%async_computation.2 | async-start | bytes 131072 | tf_op jit(solution)/shard_map/all_to_all | solution.py:101
  132.4 128.5 %reduce-scatter.2.cloned.1.call-start = ((), (), s32[]{:S(2)}) async-start(), calls=%async_computation.5 | async-start | bytes 2359296 | tf_op jit(solution)/shard_map/reduce_scatter | solution.py:156
Sparse Core Ops, SparseCore 0:
  179.4 81.4 reduce-scatter.1
where the time goes:
time: 274 us; the launch traced here: 270 us
  waiting for transfers between devices  122 us (45%)
  matrix products  64.2 us (23%)
  starting transfers between devices  30.2 us (11%)
  blocking collectives  20.8 us (8%)
  between operations  14.3 us (5%)
  other arithmetic  10.3 us (4%)
  local copies, waits for them, and re-layouts  8.05 us (3%)
    reduce_scatter x1, waiting for transfers between devices, per_device(): lax.psum_scatter(lax.dot_general(out_weight, state, (((0,), (contract,)),...  81.6 us
    dot_general x2, matrix products, hidden_rows(): jnp.dot(act_one, mid, preferred_element_type=jnp.float32) + bias[1]  32.1 us
    all_to_all x2, waiting for transfers between devices, channel_conv(): lax.all_to_all(state_cols, 'ctx', split_axis=0, concat_axis=1, tiled=True)  24.6 us
    all_to_all x1, blocking collectives, channel_conv(): return lax.all_to_all(conv, 'ctx', split_axis=1, concat_axis=0, tiled=True)  20.8 us
    all_to_all x2, starting transfers between devices, channel_conv(): lax.all_to_all(state_cols, 'ctx', split_axis=0, concat_axis=1, tiled=True)  20.8 us
    all_to_all x1, waiting for transfers between devices, channel_conv(): return lax.all_to_all(conv, 'ctx', split_axis=1, concat_axis=0, tiled=True)  15.7 us
  transfers between devices with their start and end apart: 5, of which 4 were waited for; matrix products, arithmetic and copies ran while one was open for 20% of the time, Pallas kernels for 0%

commit v1 on v0

v1 whole, which is shorter than its diff:
```python
import functools
import math

import jax
import jax.numpy as jnp
import numpy as np
from jax import lax
from jax.experimental import pallas as pl
from jax.experimental.pallas import tpu as pltpu
from jax.sharding import PartitionSpec as P

MESH = pl.DeviceIdType.MESH
BF16 = jnp.bfloat16
F32 = jnp.float32
EMB = 5
LANES = 128


def split_table(table):
    high = table.astype(np.float32).astype(jnp.bfloat16)
    low = (table - high.astype(np.float64)).astype(np.float32).astype(jnp.bfloat16)
    return np.stack([high, low])


def transform_tables(rows, kept):
    total = 2 * rows * LANES
    k = np.arange(kept)[:, None]
    live = k <= rows
    a = np.arange(rows)[None, :]
    b = np.arange(LANES)[None, :]
    angle = 2.0 * np.pi * ((k * a) % (2 * rows)) / (2 * rows)
    cos_a = np.where(live, np.cos(angle), 0.0)
    sin_a = np.where(live, np.sin(angle), 0.0)
    first = np.concatenate([cos_a, -sin_a], axis=0)
    weight = np.where((k == 0) | (k == rows), 1.0, 2.0) / total
    last = np.concatenate([(weight * cos_a).T, (-weight * sin_a).T], axis=1)
    turn = 2.0 * np.pi * ((k * b) % total) / total
    twiddle = np.stack([np.cos(turn), -np.sin(turn)]).astype(np.float32)
    j = np.arange(LANES)[:, None]
    phase = 2.0 * np.pi * ((j * b) % LANES) / LANES
    cos_b, sin_b = np.cos(phase), np.sin(phase)
    forward = np.block([[cos_b, -sin_b], [sin_b, cos_b]])
    wide = np.concatenate([split_table(forward), split_table(forward.T)])
    return split_table(first), split_table(last), twiddle, wide


def feature_table(seq_len):
    positions = np.arange(seq_len, dtype=np.int32)
    rows = [positions.astype(np.float32) / np.float32(seq_len)]
    cosines, sines = [], []
    for band in range((EMB - 1) // 2):
        wrapped = (band + 1) * positions % seq_len
        angle = np.float32(2.0 * math.pi / seq_len) * wrapped.astype(np.float32)
        cosines.append(np.cos(angle))
        sines.append(np.sin(angle))
    table = np.zeros((8, seq_len), np.float32)
    table[:EMB] = np.stack(rows + cosines + sines)
    return table.astype(jnp.bfloat16)


def sine_terms():
    e = 0.25 * np.cos(np.pi * (np.arange(400) + 0.5) / 800)
    basis = np.stack([e ** (2 * i + 1) for i in range(5)], axis=1)
    scale = 1.0 / np.maximum(np.abs(np.sin(2 * np.pi * e)), 1e-3)
    terms = np.linalg.lstsq(basis * scale[:, None], np.sin(2 * np.pi * e) * scale, rcond=None)[0]
    return [float(np.float32(t)) for t in terms]


def dot(a, b):
    return jnp.dot(a, b, preferred_element_type=F32)


def dot_nt(a, b):
    return lax.dot_general(a, b, (((1,), (1,)), ((), ())), preferred_element_type=F32)


def halves(x):
    high = x.astype(BF16)
    return high, (x - high.astype(F32)).astype(BF16)


def eye(n, dtype):
    rows = lax.broadcasted_iota(jnp.int32, (n, n), 0)
    cols = lax.broadcasted_iota(jnp.int32, (n, n), 1)
    return (rows == cols).astype(F32).astype(dtype)


def column(row, n):
    rows = lax.broadcasted_iota(jnp.int32, (n, n), 0)
    cols = lax.broadcasted_iota(jnp.int32, (n, n), 1)
    return jnp.sum(jnp.where(rows == cols, row, 0.0), axis=1, keepdims=True)


def kernel(
    n_ctx,
    n_ch,
    chunk,
    sine,
    streams_in,
    short_in,
    first_in,
    bias_in,
    mid_in,
    freq_in,
    last_in,
    decay_in,
    skip_in,
    weight_in,
    lead_in,
    tail_in,
    twiddle_in,
    wide_in,
    feat_in,
    out_ref,
    streams,
    short,
    first,
    bias,
    mid,
    freq,
    last,
    decay,
    skip,
    lead,
    tail,
    twiddle,
    wide,
    feat,
    outgoing,
    incoming,
    stage,
    signal,
    filt,
    spectrum,
    back_out,
    back_in,
    gathered,
    weight,
    load_sem,
    send_sem,
    recv_sem,
    back_send,
    back_recv,
    ring_send,
    ring_recv,
    w_send,
    w_recv,
    pair_send,
    pair_recv,
):
    me = lax.axis_index("ctx")
    group = lax.axis_index("ch")
    half = lax.rem(me, 2)
    partner = me + 1 - 2 * half
    tok, chl = streams.shape[1], streams.shape[2]
    per = chl // n_ctx
    kept = twiddle.shape[1]
    seq_len = feat.shape[1]

    def ctx_peer(d):
        return lax.rem(me + d, n_ctx)

    def ch_peer(d):
        return lax.rem(group + d, n_ch)

    barrier = pltpu.get_barrier_semaphore()

    def greet_ctx(d, carry):
        pl.semaphore_signal(barrier, inc=1, device_id=(ctx_peer(d), group), device_id_type=MESH)
        return carry

    def greet_ch(d, carry):
        pl.semaphore_signal(barrier, inc=1, device_id=(me, ch_peer(d)), device_id_type=MESH)
        return carry

    lax.fori_loop(1, n_ctx, greet_ctx, 0)
    lax.fori_loop(1, n_ch, greet_ch, 0)

    loads = []
    pairs = (
        (streams_in, streams),
        (feat_in, feat),
        (first_in, first),
        (bias_in, bias),
        (mid_in, mid),
        (freq_in, freq),
        (last_in, last),
        (decay_in, decay),
        (lead_in, lead),
        (twiddle_in, twiddle),
        (wide_in, wide),
        (short_in, short),
        (skip_in, skip),
        (tail_in, tail),
    )
    for i, (src, dst) in enumerate(pairs):
        copy = pltpu.make_async_copy(src, dst, load_sem.at[i])
        copy.start()
        loads.append(copy)

    loads[0].wait()
    flip = eye(chl, BF16)
    for s in range(3):
        stage[...] = dot_nt(flip, streams[s])
        outgoing[s] = stage[...].reshape(n_ctx, per, tok).astype(BF16)

    for copy in loads[1:]:
        copy.wait()

    lane = lax.broadcasted_iota(jnp.int32, (1, chl), 1)

    def picked(row, c):
        return jnp.sum(jnp.where(lane == me * per + c, row, 0.0), axis=1, keepdims=True)

    pick_rows = lax.broadcasted_iota(jnp.int32, (8, chl), 0)
    pick_cols = lax.broadcasted_iota(jnp.int32, (8, chl), 1)
    pick = jnp.where((pick_rows < per) & (pick_cols == me * per + pick_rows), 1.0, 0.0)

    def make_filter(o):
        hidden = mid.shape[1]
        base = first[o].astype(F32)
        base = jnp.concatenate([base, jnp.zeros((8 - EMB, hidden), F32)], axis=0).astype(BF16)
        flip_h = eye(hidden, BF16)
        lift = dot_nt(flip_h, base).astype(BF16)
        mix = dot_nt(flip_h, mid[o]).astype(BF16)
        pull = dot_nt(pick.astype(BF16), last[o]).astype(BF16)
        rate_row = jnp.where(pick > 0.0, decay[o : o + 1, :], 0.0)
        rate = jnp.sum(rate_row, axis=1, keepdims=True)
        gain = jnp.sqrt(2.0 * rate)
        turns = column(freq[o : o + 1, :], hidden) * (1.0 / (2.0 * math.pi))
        shift_one = column(bias[o, 0:1, :], hidden) * turns - 0.25
        shift_two = column(bias[o, 1:2, :], hidden) * turns - 0.25

        def sine_of(pre, shift):
            t = pre * turns + shift
            e = 0.25 - jnp.abs(t - jnp.round(t))
            e2 = e * e
            acc = sine[-1]
            for term in sine[-2::-1]:
                acc = acc * e2 + term
            return (acc * e).astype(BF16)

        def step(i, carry):
            start = pl.multiple_of(i * chunk, chunk)
            act_one = sine_of(dot(lift, feat[:, pl.ds(start, chunk)]), shift_one)
            act_two = sine_of(dot(mix, act_one), shift_two)
            raw = dot(pull, act_two)
            lag = (lax.broadcasted_iota(jnp.int32, (8, chunk), 1) + start).astype(F32)
            value = raw * jnp.exp(-rate * lag) * gain
            for q in range(chunk // LANES):
                row = pl.multiple_of((i * (chunk // LANES) + q) * 8, 8)
                filt[pl.ds(row, 8), :] = value[:, q * LANES : (q + 1) * LANES]
            return carry

        lax.fori_loop(0, seq_len // chunk, step, 0)

    tw_re, tw_im = twiddle[0], twiddle[1]

    def forward(terms):
        high = terms[0]
        part = dot(lead[0], high) + dot(lead[1], high)
        if len(terms) > 1:
            part = part + dot(lead[0], terms[1])
        rows = []
        for c in range(per):
            re = part[:kept, c * LANES : (c + 1) * LANES]
            im = part[kept:, c * LANES : (c + 1) * LANES]
            rows.append(jnp.concatenate([re * tw_re - im * tw_im, re * tw_im + im * tw_re], axis=1))
        high, low = halves(jnp.concatenate(rows, axis=0))
        return dot(high, wide[0]) + dot(low, wide[0]) + dot(high, wide[1])

    def inverse(spec):
        high, low = halves(spec)
        part = dot(high, wide[2]) + dot(low, wide[2]) + dot(high, wide[3])
        cols = []
        for c in range(per):
            re = part[c * kept : (c + 1) * kept, :LANES]
            im = part[c * kept : (c + 1) * kept, LANES:]
            cols.append(jnp.concatenate([re * tw_re + im * tw_im, im * tw_re - re * tw_im], axis=0))
        high, low = halves(jnp.concatenate(cols, axis=1))
        return dot(tail[0], high) + dot(tail[0], low) + dot(tail[1], high)

    def make_spectrum(o):
        cols = [filt[pl.ds(c, n_ctx, stride=8), :] for c in range(per)]
        spectrum[o] = forward(halves(jnp.concatenate(cols, axis=1)))

    def convolve(o, state):
        spec = forward((state.astype(BF16),))
        re, im = spec[:, :LANES], spec[:, LANES:]
        f_re, f_im = spectrum[o, :, :LANES], spectrum[o, :, LANES:]
        return inverse(jnp.concatenate([re * f_re - im * f_im, re * f_im + im * f_re], axis=1))

    make_filter(0)
    make_spectrum(0)
    pl.semaphore_wait(barrier, n_ctx + n_ch - 2)

    for s in range(3):
        pltpu.make_async_copy(outgoing.at[s, me], incoming.at[s, me], recv_sem.at[s]).start()

        def send(d, carry):
            peer = ctx_peer(d)
            pltpu.make_async_remote_copy(
                src_ref=outgoing.at[s, peer],
                dst_ref=incoming.at[s, me],
                send_sem=send_sem.at[s],
                recv_sem=recv_sem.at[s],
                device_id=(peer, group),
                device_id_type=MESH,
            ).start()
            return carry

        lax.fori_loop(1, n_ctx, send, 0)

    depth, cols_out = weight.shape[2], weight.shape[3]

    def weight_block(g):
        return weight_in.at[
            pl.ds(pl.multiple_of(half * depth, depth), depth),
            pl.ds(pl.multiple_of(g * cols_out, cols_out), cols_out),
        ]

    pltpu.make_async_copy(weight_block(group), weight.at[group, half], w_recv).start()

    def send_weight(d, carry):
        peer = ch_peer(d)
        pltpu.make_async_remote_copy(
            src_ref=weight_block(peer),
            dst_ref=weight.at[group, half],
            send_sem=w_send,
            recv_sem=w_recv,
            device_id=(me, peer),
            device_id_type=MESH,
        ).start()
        return carry

    lax.fori_loop(1, n_ch, send_weight, 0)

    make_filter(1)
    make_spectrum(1)

    row0 = lax.broadcasted_iota(jnp.int32, (n_ctx, LANES), 0) == 0
    lane_at = lax.broadcasted_iota(jnp.int32, (n_ctx, LANES), 1)

    def delayed(x, by):
        near = pltpu.roll(x, by, 1)
        carried = jnp.where(row0, 0.0, pltpu.roll(near, 1, 0))
        return jnp.where(lane_at < by, carried, near)

    def shortened(s):
        pltpu.make_async_copy(incoming.at[s], incoming.at[s], recv_sem.at[s]).wait()
        signal[...] = incoming[s].astype(F32).reshape(n_ctx * per, tok)
        cols = []
        for c in range(per):
            x = signal[pl.ds(c, n_ctx, stride=per), :]
            taps = [picked(short[s, i : i + 1, :], c) for i in range(3)]
            cols.append(taps[0] * x + taps[1] * delayed(x, 1) + taps[2] * delayed(x, 2))
        return jnp.concatenate(cols, axis=1).astype(BF16).astype(F32)

    state = shortened(0)
    for o in range(2):
        direct = jnp.concatenate(
            [jnp.broadcast_to(picked(skip[o : o + 1, :], c), (1, LANES)) for c in range(per)], axis=1
        )
        output = convolve(o, state) + direct * state
        state = (shortened(o + 1) * output).astype(BF16).astype(F32)
    for c in range(per):
        stage[pl.ds(c, n_ctx, stride=per), :] = state[:, c * LANES : (c + 1) * LANES]
    back_out[...] = stage[...].reshape(n_ctx, per, tok).astype(BF16)

    pltpu.make_async_copy(back_out.at[me], back_in.at[me], back_recv).start()

    def send_back(d, carry):
        peer = ctx_peer(d)
        pltpu.make_async_remote_copy(
            src_ref=back_out.at[peer],
            dst_ref=back_in.at[me],
            send_sem=back_send,
            recv_sem=back_recv,
            device_id=(peer, group),
            device_id_type=MESH,
        ).start()
        return carry

    lax.fori_loop(1, n_ctx, send_back, 0)

    pltpu.make_async_copy(weight.at[:, half], weight.at[:, half], w_recv).wait()
    swap = pltpu.make_async_remote_copy(
        src_ref=weight.at[:, half],
        dst_ref=weight.at[:, half],
        send_sem=pair_send,
        recv_sem=pair_recv,
        device_id=(partner, group),
        device_id_type=MESH,
    )
    swap.start()

    pltpu.make_async_copy(back_in, back_in, back_recv).wait()
    signal[...] = back_in[...].astype(F32).reshape(n_ctx * per, tok)
    mine = dot_nt(eye(tok, BF16), signal[...].astype(BF16)).astype(BF16)
    gathered[group] = mine

    def send_ring(d, carry):
        pltpu.make_async_remote_copy(
            src_ref=gathered.at[group],
            dst_ref=gathered.at[group],
            send_sem=ring_send,
            recv_sem=ring_recv.at[group],
            device_id=(me, ch_peer(d)),
            device_id_type=MESH,
        ).start()
        return carry

    lax.fori_loop(1, n_ch, send_ring, 0)
    swap.wait()

    def product(g, rows):
        return dot(rows, weight[g].reshape(2 * depth, cols_out))

    total = product(group, mine)
    for d in range(1, n_ch):
        peer = ch_peer(d)
        pltpu.make_async_copy(gathered.at[peer], gathered.at[peer], ring_recv.at[peer]).wait()
        total = total + product(peer, gathered[peer])
    out_ref[...] = total.astype(BF16)

    for s in range(3):
        sent = outgoing.at[s, pl.ds(0, n_ctx - 1)]
        pltpu.make_async_copy(sent, sent, send_sem.at[s]).wait()
    sent = back_out.at[pl.ds(0, n_ctx - 1)]
    pltpu.make_async_copy(sent, sent, back_send).wait()
    sent = gathered.at[pl.ds(0, n_ch - 1)]
    pltpu.make_async_copy(sent, sent, ring_send).wait()
    sent = weight.at[pl.ds(0, n_ch - 1), half]
    pltpu.make_async_copy(sent, sent, w_send).wait()


def solution(mesh):
    n_ctx, n_ch = mesh.shape["ctx"], mesh.shape["ch"]

    def per_device(
        streams,
        short_weight,
        filt_first,
        filt_bias,
        filt_mid,
        filt_freq,
        filt_last,
        decay,
        skip,
        out_weight,
    ):
        tok, chl = streams.shape[1], streams.shape[2]
        per = chl // n_ctx
        seq_len = tok * n_ctx
        kept = (n_ctx + 1 + 7) // 8 * 8
        cols_out = out_weight.shape[1] // n_ch
        lead, tail, twiddle, wide = transform_tables(n_ctx, kept)
        feat = feature_table(seq_len)
        args = (
            streams,
            short_weight,
            filt_first,
            filt_bias,
            filt_mid,
            filt_freq,
            filt_last,
            decay,
            skip,
            out_weight,
            jnp.asarray(lead),
            jnp.asarray(tail),
            jnp.asarray(twiddle),
            jnp.asarray(wide),
            jnp.asarray(feat),
        )

        def vmem(x):
            return pltpu.VMEM(x.shape, x.dtype)

        staged = [vmem(args[i]) for i in (0, 1, 2, 3, 4, 5, 6, 7, 8, 10, 11, 12, 13, 14)]
        dma = pltpu.SemaphoreType.DMA
        return pl.pallas_call(
            functools.partial(kernel, n_ctx, n_ch, min(1024, seq_len), sine_terms()),
            out_shape=jax.ShapeDtypeStruct((tok, cols_out), BF16),
            in_specs=[pl.BlockSpec(memory_space=pl.ANY)] * len(args),
            out_specs=pl.BlockSpec(memory_space=pltpu.VMEM),
            scratch_shapes=staged
            + [
                pltpu.VMEM((3, n_ctx, per, tok), BF16),
                pltpu.VMEM((3, n_ctx, per, tok), BF16),
                pltpu.VMEM((chl, tok), F32),
                pltpu.VMEM((chl, tok), F32),
                pltpu.VMEM((n_ctx * 8, LANES), F32),
                pltpu.VMEM((2, per * kept, 2 * LANES), F32),
                pltpu.VMEM((n_ctx, per, tok), BF16),
                pltpu.VMEM((n_ctx, per, tok), BF16),
                pltpu.VMEM((n_ch, tok, chl), BF16),
                pltpu.VMEM((n_ch, 2, chl // 2, cols_out), BF16),
                dma((14,)),
                dma((3,)),
                dma((3,)),
                dma,
                dma,
                dma,
                dma((n_ch,)),
                dma,
                dma,
                dma,
                dma,
            ],
            compiler_params=pltpu.CompilerParams(collective_id=0, has_side_effects=True),
        )(*args)

    return jax.shard_map(
        per_device,
        mesh=mesh,
        in_specs=(
            P(None, "ctx", "ch"),
            P(None, None, "ch"),
            P(),
            P(),
            P(),
            P(),
            P(None, None, "ch"),
            P(None, "ch"),
            P(None, "ch"),
            P("ch", None),
        ),
        out_specs=P("ctx", "ch"),
        check_vma=False,
    )
```

time: 274 us -> 54.1 us (0.20); the launches traced: 270 us -> 53.9 us
  waiting for transfers between devices: 122 us -> 0 us
  matrix products: 64.2 us -> 0 us
  Pallas kernels: 0 us -> 51 us
  starting transfers between devices: 30.2 us -> 0 us
  blocking collectives: 20.8 us -> 0 us
  between operations: 14.3 us -> 0.01 us
  other arithmetic: 10.3 us -> 0 us
  local copies, waits for them, and re-layouts: 8.05 us -> 2.85 us
    reduce_scatter x1 -> x0, waiting for transfers between devices: 81.6 us -> none  [per_device(): lax.psum_scatter(lax.dot_general(out_weight, state, (((0,), (contract,)),...]
    dot_general x41 -> x0, matrix products: 64.2 us -> none  [the longest x2 32.1 us: hidden_rows(): jnp.dot(act_one, mid, preferred_element_type=jnp.float32) + bias[1]]
    pallas_call x0 -> x1, Pallas kernels: none -> 51 us  [per_device(): pl.pallas_call(functools.partial(kernel, n_ctx, n_ch, min(1024, seq_len),...]
    all_to_all x3 -> x0, waiting for transfers between devices: 40.3 us -> none  [the longest x2 24.6 us: channel_conv(): lax.all_to_all(state_cols, 'ctx', split_axis=0, concat_axis=1, tiled=True)]
    all_to_all x3 -> x0, starting transfers between devices: 25.2 us -> none  [the longest x2 20.8 us: channel_conv(): lax.all_to_all(state_cols, 'ctx', split_axis=0, concat_axis=1, tiled=True)]
    all_to_all x1 -> x0, blocking collectives: 20.8 us -> none  [channel_conv(): return lax.all_to_all(conv, 'ctx', split_axis=1, concat_axis=0, tiled=True)]
    ppermute x1 -> x0, starting transfers between devices: 4.91 us -> none  [shifted(): return lax.ppermute(x, axis, pairs)]
    convert_element_type x4 -> x0, other arithmetic: 4.34 us -> none  [the longest x1 1.62 us: per_device(): return share.T.astype(jnp.bfloat16)]
  transfers between devices with their start and end apart: 5 -> 0, of which waited for: 4 -> 0; matrix products, arithmetic and copies ran while one was open for 20% -> 0% of each run, Pallas kernels for 0% -> 0%
where the time goes in v1:
time: 54.1 us; the launch traced here: 53.9 us
  Pallas kernels  51 us (94%)
  local copies, waits for them, and re-layouts  2.85 us (5%)
    pallas_call x1, Pallas kernels, per_device(): pl.pallas_call(functools.partial(kernel, n_ctx, n_ch, min(1024, seq_len),...  51 us
    unnamed x2, local copies, waits for them, and re-layouts  2.85 us

profile of v1, /device:TPU:1, one launch (start us, length us, event | category | flops | bytes accessed | tf_op | source)
XLA Modules:
  0.0 53.9 jit_solution(17001213399930510284)
XLA Ops:
  0.0 1.3 %copy.16.first_in = bf16[2,5,64]{2,1,0:T(8,128)(2,1)} copy(bf16[2,5,64]{2,0,1:T(2,128)(2,1)} %param.17) | data formatting | bytes 2560 | tf_op args[2]
  1.3 51.0 %shard_map.145 = bf16[128,512]{1,0:T(8,128)(2,1)} custom-call(bf16[3,128,256]{2,1,0:T(8,128)(2,1)} %streams_in.1, f32[3,3,256]{2,1,0:T(4,128)} %short_in.1, bf16[2,5,64]{2,1,0:T(8,128)(2,1)} %copy.16.first_in, f32[2,2,64]{2,1,0:T(2,128)} %bias_in.1, bf16[2,64,64]{2,1,0:T(8,128)(2,1)} %mid_in.1, f32[2,64]{1,0:T(2,128)} %freq_in.1, ...), custom_call_target="tpu_custom_call" | custom-call | tf_op jit(solution)/shard_map/pallas_call | solution.py:482
  52.3 1.6 %copy.18 = bf16[128,512]{1,0:T(8,128)(2,1)} copy(bf16[128,512]{1,0:T(8,128)(2,1)} %shard_map.145) | data formatting | bytes 262144

commit v2 on v1

v2 whole, which is shorter than its diff:
```python
import functools
import math

import jax
import jax.numpy as jnp
import numpy as np
from jax import lax
from jax.experimental import pallas as pl
from jax.experimental.pallas import tpu as pltpu
from jax.sharding import PartitionSpec as P

MESH = pl.DeviceIdType.MESH
BF16 = jnp.bfloat16
F32 = jnp.float32
EMB = 5
LANES = 128


def split_table(table):
    high = table.astype(np.float32).astype(jnp.bfloat16)
    low = (table - high.astype(np.float64)).astype(np.float32).astype(jnp.bfloat16)
    return np.stack([high, low])


def transform_tables(rows, kept):
    total = 2 * rows * LANES
    k = np.arange(kept)[:, None]
    live = k <= rows
    a = np.arange(rows)[None, :]
    b = np.arange(LANES)[None, :]
    angle = 2.0 * np.pi * ((k * a) % (2 * rows)) / (2 * rows)
    cos_a = np.where(live, np.cos(angle), 0.0)
    sin_a = np.where(live, np.sin(angle), 0.0)
    first = np.concatenate([cos_a, -sin_a], axis=0)
    weight = np.where((k == 0) | (k == rows), 1.0, 2.0) / total
    last = np.concatenate([(weight * cos_a).T, (-weight * sin_a).T], axis=1)
    turn = 2.0 * np.pi * ((k * b) % total) / total
    twiddle = np.stack([np.cos(turn), -np.sin(turn)]).astype(np.float32)
    j = np.arange(LANES)[:, None]
    phase = 2.0 * np.pi * ((j * b) % LANES) / LANES
    cos_b, sin_b = np.cos(phase), np.sin(phase)
    forward = np.block([[cos_b, -sin_b], [sin_b, cos_b]])
    wide = np.concatenate([split_table(forward), split_table(forward.T)])
    return split_table(first), split_table(last), twiddle, wide


def feature_table(seq_len):
    positions = np.arange(seq_len, dtype=np.int32)
    rows = [positions.astype(np.float32) / np.float32(seq_len)]
    cosines, sines = [], []
    for band in range((EMB - 1) // 2):
        wrapped = (band + 1) * positions % seq_len
        angle = np.float32(2.0 * math.pi / seq_len) * wrapped.astype(np.float32)
        cosines.append(np.cos(angle))
        sines.append(np.sin(angle))
    table = np.zeros((8, seq_len), np.float32)
    table[:EMB] = np.stack(rows + cosines + sines)
    table[EMB] = 1.0
    return np.concatenate([table] * 3).astype(jnp.bfloat16)


def sine_terms():
    e = 0.25 * np.cos(np.pi * (np.arange(400) + 0.5) / 800)
    basis = np.stack([e ** (2 * i + 1) for i in range(4)], axis=1)
    scale = 1.0 / np.maximum(np.abs(np.sin(2 * np.pi * e)), 1e-3)
    terms = np.linalg.lstsq(basis * scale[:, None], np.sin(2 * np.pi * e) * scale, rcond=None)[0]
    return [float(np.float32(t)) for t in terms]


def dot(a, b):
    return jnp.dot(a, b, preferred_element_type=F32)


def dot_nt(a, b):
    return lax.dot_general(a, b, (((1,), (1,)), ((), ())), preferred_element_type=F32)


def halves(x):
    high = x.astype(BF16)
    return high, (x - high.astype(F32)).astype(BF16)


def eye(n, dtype):
    rows = lax.broadcasted_iota(jnp.int32, (n, n), 0)
    cols = lax.broadcasted_iota(jnp.int32, (n, n), 1)
    return (rows == cols).astype(F32).astype(dtype)


def terms(x, count):
    parts = []
    for _ in range(count):
        part = x.astype(BF16).astype(F32)
        parts.append(part)
        x = x - part
    return parts


def kernel(
    n_ctx,
    n_ch,
    chunk,
    sine,
    streams_in,
    short_in,
    first_in,
    bias_in,
    mid_in,
    freq_in,
    last_in,
    decay_in,
    skip_in,
    weight_in,
    lead_in,
    tail_in,
    twiddle_in,
    wide_in,
    feat_in,
    out_ref,
    streams,
    short,
    first,
    bias,
    mid,
    freq,
    last,
    decay,
    skip,
    lead,
    tail,
    twiddle,
    wide,
    feat,
    outgoing,
    incoming,
    signal,
    filt,
    spectrum,
    back_out,
    back_in,
    gathered,
    weight,
    load_sem,
    send_sem,
    recv_sem,
    back_send,
    back_recv,
    ring_send,
    ring_recv,
    w_send,
    w_recv,
    pair_send,
    pair_recv,
    filt_send,
    filt_recv,
):
    me = lax.axis_index("ctx")
    group = lax.axis_index("ch")
    half = lax.rem(me, 2)
    partner = me + 1 - 2 * half
    tok, chl = streams.shape[1], streams.shape[2]
    wide_half = chl // 2
    kept = twiddle.shape[1]
    seq_len = feat.shape[1]

    def ctx_peer(d):
        return lax.rem(me + d, n_ctx)

    def ch_peer(d):
        return lax.rem(group + d, n_ch)

    def for_ctx_peers(act):
        quarter = n_ctx // 4
        act(ctx_peer(quarter))
        act(ctx_peer(3 * quarter))

        def step(e, carry):
            act(ctx_peer(quarter + e))
            act(ctx_peer(quarter - e))
            act(ctx_peer(3 * quarter + e))
            act(ctx_peer(3 * quarter - e))
            return carry

        lax.fori_loop(1, quarter, step, 0)
        act(ctx_peer(2 * quarter))

    loads = []
    pairs = (
        (streams_in, streams),
        (feat_in, feat),
        (first_in, first),
        (bias_in, bias),
        (mid_in, mid),
        (freq_in, freq),
        (last_in, last),
        (decay_in, decay),
        (lead_in, lead),
        (twiddle_in, twiddle),
        (wide_in, wide),
        (short_in, short),
        (skip_in, skip),
        (tail_in, tail),
    )
    for i, (src, dst) in enumerate(pairs):
        copy = pltpu.make_async_copy(src, dst, load_sem.at[i])
        copy.start()
        loads.append(copy)

    barrier = pltpu.get_barrier_semaphore()

    def greet_ctx(peer):
        pl.semaphore_signal(barrier, inc=1, device_id=(peer, group), device_id_type=MESH)

    for_ctx_peers(greet_ctx)
    for d in range(1, n_ch):
        pl.semaphore_signal(barrier, inc=1, device_id=(me, ch_peer(d)), device_id_type=MESH)

    loads[0].wait()
    flip = eye(tok, BF16)
    for h in range(2):
        for s in range(3):
            block = streams[s, :, h * wide_half : (h + 1) * wide_half]
            turned = dot_nt(eye(wide_half, BF16), block)
            outgoing[h, :, s] = turned.reshape(n_ctx, 2, tok).astype(BF16)

    pl.semaphore_wait(barrier, n_ctx + n_ch - 2)

    for h in range(2):
        pltpu.make_async_copy(outgoing.at[h, me], incoming.at[h, me], recv_sem.at[h]).start()

        def send(peer):
            pltpu.make_async_remote_copy(
                src_ref=outgoing.at[h, peer],
                dst_ref=incoming.at[h, me],
                send_sem=send_sem.at[h],
                recv_sem=recv_sem.at[h],
                device_id=(peer, group),
                device_id_type=MESH,
            ).start()

        for_ctx_peers(send)

    depth, cols_out = weight.shape[2], weight.shape[3]

    def weight_block(g):
        return weight_in.at[
            pl.ds(pl.multiple_of(half * depth, depth), depth),
            pl.ds(pl.multiple_of(g * cols_out, cols_out), cols_out),
        ]

    pltpu.make_async_copy(weight_block(group), weight.at[group, half], w_recv).start()
    for d in range(1, n_ch):
        pltpu.make_async_remote_copy(
            src_ref=weight_block(ch_peer(d)),
            dst_ref=weight.at[group, half],
            send_sem=w_send,
            recv_sem=w_recv,
            device_id=(me, ch_peer(d)),
            device_id_type=MESH,
        ).start()

    for copy in loads[1:]:
        copy.wait()

    lane = lax.broadcasted_iota(jnp.int32, (1, chl), 1)

    def place(owner, c):
        return (c // 2) * wide_half + 2 * owner + c % 2

    def picked(row, c):
        return jnp.sum(jnp.where(lane == place(me, c), row, 0.0), axis=1, keepdims=True)

    pick_rows = lax.broadcasted_iota(jnp.int32, (8, chl), 0)
    pick_cols = lax.broadcasted_iota(jnp.int32, (8, chl), 1)
    pick = jnp.zeros((8, chl), F32)
    for r in range(8):
        here = (pick_rows == r) & (pick_cols == place(me - half + r // 4, r % 4))
        pick = jnp.where(here, 1.0, pick)

    hidden = mid.shape[1]
    turns = freq[pl.ds(half, 1), :] * (1.0 / (2.0 * math.pi))
    both = first[...].astype(F32)
    base = jnp.where(half == 0, both[:, 0, :], both[:, 1, :]) * turns
    shifts = bias[half] * turns - 0.25
    base = jnp.concatenate([base, shifts[0:1], jnp.zeros((8 - EMB - 1, hidden), F32)], axis=0)
    flip_h = eye(hidden, BF16)
    lift = dot_nt(flip_h, jnp.concatenate(terms(base, 3), axis=0).astype(BF16)).astype(BF16)
    mixed = terms(mid[half].astype(F32) * turns, 2)
    mixed = mixed + terms(shifts[1:2], 3) + [jnp.zeros((13, hidden), F32)]
    mix = dot_nt(flip_h, jnp.concatenate(mixed, axis=0).astype(BF16)).astype(BF16)
    pull = dot_nt(pick.astype(BF16), last[half]).astype(BF16)
    rate_row = jnp.where(pick > 0.0, decay[pl.ds(half, 1), :], 0.0)
    rate = jnp.sum(rate_row, axis=1, keepdims=True)
    gain = jnp.sqrt(2.0 * rate)
    ones = (lax.broadcasted_iota(jnp.int32, (16, chunk), 0) < 3).astype(F32).astype(BF16)

    def sine_of(t):
        e = 0.25 - jnp.abs(t - jnp.round(t))
        e2 = e * e
        acc = sine[-1]
        for term in sine[-2::-1]:
            acc = acc * e2 + term
        return (acc * e).astype(BF16)

    def filter_step(i, carry):
        start = pl.multiple_of(i * chunk, chunk)
        act_one = sine_of(dot(lift, feat[:, pl.ds(start, chunk)]))
        act_two = sine_of(dot(mix, jnp.concatenate([act_one, act_one, ones], axis=0)))
        raw = dot(pull, act_two)
        lag = (lax.broadcasted_iota(jnp.int32, (8, chunk), 1) + start).astype(F32)
        value = raw * jnp.exp(-rate * lag) * gain
        for q in range(chunk // LANES):
            row = pl.multiple_of((i * (chunk // LANES) + q) * 8, 8)
            filt[half, pl.ds(row, 8), :] = value[:, q * LANES : (q + 1) * LANES]
        part = filt.at[half, pl.ds(pl.multiple_of(i * (chunk // 16), chunk // 16), chunk // 16)]
        pltpu.make_async_remote_copy(
            src_ref=part,
            dst_ref=part,
            send_sem=filt_send,
            recv_sem=filt_recv,
            device_id=(partner, group),
            device_id_type=MESH,
        ).start()
        return carry

    lax.fori_loop(0, seq_len // chunk, filter_step, 0)

    tw_re, tw_im = twiddle[0], twiddle[1]

    def forward(parts):
        high = parts[0]
        part = dot(lead[0], high) + dot(lead[1], high)
        if len(parts) > 1:
            part = part + dot(lead[0], parts[1])
        rows = []
        for c in range(high.shape[1] // LANES):
            re = part[:kept, c * LANES : (c + 1) * LANES]
            im = part[kept:, c * LANES : (c + 1) * LANES]
            rows.append(jnp.concatenate([re * tw_re - im * tw_im, re * tw_im + im * tw_re], axis=1))
        high, low = halves(jnp.concatenate(rows, axis=0))
        return dot(high, wide[0]) + dot(low, wide[0]) + dot(high, wide[1])

    def inverse(spec):
        high, low = halves(spec)
        part = dot(high, wide[2]) + dot(low, wide[2]) + dot(high, wide[3])
        cols = []
        for c in range(spec.shape[0] // kept):
            re = part[c * kept : (c + 1) * kept, :LANES]
            im = part[c * kept : (c + 1) * kept, LANES:]
            cols.append(jnp.concatenate([re * tw_re + im * tw_im, im * tw_re - re * tw_im], axis=0))
        high, low = halves(jnp.concatenate(cols, axis=1))
        return dot(tail[0], high) + dot(tail[0], low) + dot(tail[1], high)

    def make_spectrum(o):
        cols = [filt[o, pl.ds(4 * half + c, n_ctx, stride=8), :] for c in range(4)]
        spectrum[o] = forward(halves(jnp.concatenate(cols, axis=1)))

    make_spectrum(half)
    sent = filt.at[half]
    pltpu.make_async_copy(sent, sent, filt_send).wait()
    came = filt.at[1 - half]
    pltpu.make_async_copy(came, came, filt_recv).wait()
    make_spectrum(1 - half)

    def convolve(o, h, state):
        spec = forward((state.astype(BF16),))
        re, im = spec[:, :LANES], spec[:, LANES:]
        rows = slice(2 * h * kept, 2 * (h + 1) * kept)
        f_re, f_im = spectrum[o, rows, :LANES], spectrum[o, rows, LANES:]
        return inverse(jnp.concatenate([re * f_re - im * f_im, re * f_im + im * f_re], axis=1))

    row0 = lax.broadcasted_iota(jnp.int32, (n_ctx, LANES), 0) == 0
    lane_at = lax.broadcasted_iota(jnp.int32, (n_ctx, LANES), 1)

    def delayed(x, by):
        near = pltpu.roll(x, by, 1)
        carried = jnp.where(row0, 0.0, pltpu.roll(near, 1, 0))
        return jnp.where(lane_at < by, carried, near)

    def shortened(h, s):
        signal[h, s] = incoming[h, :, s].astype(F32).reshape(n_ctx * 2, tok)
        cols = []
        for c in range(2):
            x = signal[h, s, pl.ds(c, n_ctx, stride=2), :]
            taps = [picked(short[s, i : i + 1, :], 2 * h + c) for i in range(3)]
            cols.append(taps[0] * x + taps[1] * delayed(x, 1) + taps[2] * delayed(x, 2))
        return jnp.concatenate(cols, axis=1).astype(BF16).astype(F32)

    for h in range(2):
        pltpu.make_async_copy(incoming.at[h], incoming.at[h], recv_sem.at[h]).wait()
        state = shortened(h, 0)
        for o in range(2):
            direct = jnp.concatenate(
                [jnp.broadcast_to(picked(skip[o : o + 1, :], 2 * h + c), (1, LANES)) for c in range(2)],
                axis=1,
            )
            output = convolve(o, h, state) + direct * state
            state = (shortened(h, o + 1) * output).astype(BF16).astype(F32)
        for c in range(2):
            signal[h, 0, pl.ds(c, n_ctx, stride=2), :] = state[:, c * LANES : (c + 1) * LANES]
        back_out[h] = signal[h, 0].reshape(n_ctx, 2, tok).astype(BF16)

        pltpu.make_async_copy(back_out.at[h, me], back_in.at[h, me], back_recv.at[h]).start()

        def send_back(peer):
            pltpu.make_async_remote_copy(
                src_ref=back_out.at[h, peer],
                dst_ref=back_in.at[h, me],
                send_sem=back_send.at[h],
                recv_sem=back_recv.at[h],
                device_id=(peer, group),
                device_id_type=MESH,
            ).start()

        for_ctx_peers(send_back)

    pltpu.make_async_copy(weight.at[:, half], weight.at[:, half], w_recv).wait()
    swap = pltpu.make_async_remote_copy(
        src_ref=weight.at[:, half],
        dst_ref=weight.at[:, half],
        send_sem=pair_send,
        recv_sem=pair_recv,
        device_id=(partner, group),
        device_id_type=MESH,
    )
    swap.start()

    for h in range(2):
        pltpu.make_async_copy(back_in.at[h], back_in.at[h], back_recv.at[h]).wait()
        block = back_in[h].astype(F32).reshape(n_ctx * 2, tok)
        gathered[h, group] = dot_nt(flip, block.astype(BF16)).astype(BF16)
        for d in range(1, n_ch):
            pltpu.make_async_remote_copy(
                src_ref=gathered.at[h, group],
                dst_ref=gathered.at[h, group],
                send_sem=ring_send.at[h],
                recv_sem=ring_recv.at[h, group],
                device_id=(me, ch_peer(d)),
                device_id_type=MESH,
            ).start()

    swap.wait()

    total = jnp.zeros((tok, cols_out), F32)
    for h in range(2):
        for d in range(n_ch):
            peer = ch_peer(d)
            if d > 0:
                came = gathered.at[h, peer]
                pltpu.make_async_copy(came, came, ring_recv.at[h, peer]).wait()
            total = total + dot(gathered[h, peer], weight[peer, h])
    out_ref[...] = total.astype(BF16)

    for h in range(2):
        sent = outgoing.at[h, pl.ds(0, n_ctx - 1)]
        pltpu.make_async_copy(sent, sent, send_sem.at[h]).wait()
        sent = back_out.at[h, pl.ds(0, n_ctx - 1)]
        pltpu.make_async_copy(sent, sent, back_send.at[h]).wait()
        sent = gathered.at[h, pl.ds(0, n_ch - 1)]
        pltpu.make_async_copy(sent, sent, ring_send.at[h]).wait()
    sent = weight.at[pl.ds(0, n_ch - 1), half]
    pltpu.make_async_copy(sent, sent, w_send).wait()


def solution(mesh):
    n_ctx, n_ch = mesh.shape["ctx"], mesh.shape["ch"]

    def per_device(
        streams,
        short_weight,
        filt_first,
        filt_bias,
        filt_mid,
        filt_freq,
        filt_last,
        decay,
        skip,
        out_weight,
    ):
        tok, chl = streams.shape[1], streams.shape[2]
        seq_len = tok * n_ctx
        kept = (n_ctx + 1 + 7) // 8 * 8
        cols_out = out_weight.shape[1] // n_ch
        lead, tail, twiddle, wide = transform_tables(n_ctx, kept)
        feat = feature_table(seq_len)
        args = (
            streams,
            short_weight,
            jnp.transpose(filt_first, (1, 0, 2)),
            filt_bias,
            filt_mid,
            filt_freq,
            filt_last,
            decay,
            skip,
            out_weight,
            jnp.asarray(lead),
            jnp.asarray(tail),
            jnp.asarray(twiddle),
            jnp.asarray(wide),
            jnp.asarray(feat),
        )

        def vmem(x):
            return pltpu.VMEM(x.shape, x.dtype)

        staged = [vmem(args[i]) for i in (0, 1, 2, 3, 4, 5, 6, 7, 8, 10, 11, 12, 13, 14)]
        dma = pltpu.SemaphoreType.DMA
        return pl.pallas_call(
            functools.partial(kernel, n_ctx, n_ch, min(512, seq_len), sine_terms()),
            out_shape=jax.ShapeDtypeStruct((tok, cols_out), BF16),
            in_specs=[pl.BlockSpec(memory_space=pl.ANY)] * len(args),
            out_specs=pl.BlockSpec(memory_space=pltpu.VMEM),
            scratch_shapes=staged
            + [
                pltpu.VMEM((2, n_ctx, 3, 2, tok), BF16),
                pltpu.VMEM((2, n_ctx, 3, 2, tok), BF16),
                pltpu.VMEM((2, 3, n_ctx * 2, tok), F32),
                pltpu.VMEM((2, n_ctx * 8, LANES), F32),
                pltpu.VMEM((2, 4 * kept, 2 * LANES), F32),
                pltpu.VMEM((2, n_ctx, 2, tok), BF16),
                pltpu.VMEM((2, n_ctx, 2, tok), BF16),
                pltpu.VMEM((2, n_ch, tok, chl // 2), BF16),
                pltpu.VMEM((n_ch, 2, chl // 2, cols_out), BF16),
                dma((14,)),
                dma((2,)),
                dma((2,)),
                dma((2,)),
                dma((2,)),
                dma((2,)),
                dma((2, n_ch)),
                dma,
                dma,
                dma,
                dma,
                dma,
                dma,
            ],
            compiler_params=pltpu.CompilerParams(collective_id=0, has_side_effects=True),
        )(*args)

    return jax.shard_map(
        per_device,
        mesh=mesh,
        in_specs=(
            P(None, "ctx", "ch"),
            P(None, None, "ch"),
            P(),
            P(),
            P(),
            P(),
            P(None, None, "ch"),
            P(None, "ch"),
            P(None, "ch"),
            P("ch", None),
        ),
        out_specs=P("ctx", "ch"),
        check_vma=False,
    )
```

time: 54.1 us -> 48.1 us (0.89)
  Pallas kernels: 51 us -> 46.3 us
  local copies, waits for them, and re-layouts: 2.85 us -> 1.57 us
    pallas_call x1, Pallas kernels: 51 us -> 46.3 us  [per_device(): pl.pallas_call(functools.partial(kernel, n_ctx, n_ch, min(512, seq_len),...]
    unnamed x2 -> x1, local copies, waits for them, and re-layouts: 2.85 us -> 1.57 us
where the time goes in v2:
time: 48.1 us; the launch traced here: 47.9 us
  Pallas kernels  46.3 us (96%)
  local copies, waits for them, and re-layouts  1.57 us (3%)
    pallas_call x1, Pallas kernels, per_device(): pl.pallas_call(functools.partial(kernel, n_ctx, n_ch, min(512, seq_len),...  46.3 us
    unnamed x1, local copies, waits for them, and re-layouts  1.57 us

profile of v2, /device:TPU:1, one launch (start us, length us, event | category | flops | bytes accessed | tf_op | source)
XLA Modules:
  0.0 47.9 jit_solution(1670544801104877591)
XLA Ops:
  0.0 46.3 %shard_map.145 = bf16[128,512]{1,0:T(8,128)(2,1)} custom-call(bf16[3,128,256]{2,1,0:T(8,128)(2,1)} %streams_in.1, f32[3,3,256]{2,1,0:T(4,128)} %short_in.1, bf16[5,2,64]{2,1,0:T(2,128)(2,1)} %bitcast.1, f32[2,2,64]{2,1,0:T(2,128)} %bias_in.1, bf16[2,64,64]{2,1,0:T(8,128)(2,1)} %mid_in.1, f32[2,64]{1,0:T(2,128)} %freq_in.1, bf16[2,64,256]{2,1,0:T(8,128)(2,1)} %last_in.1, ...), custom_call_target="tpu_custom_call" | custom-call | tf_op jit(solution)/shard_map/pallas_call | solution.py:508
  46.3 1.6 %copy.17 = bf16[128,512]{1,0:T(8,128)(2,1)} copy(bf16[128,512]{1,0:T(8,128)(2,1)} %shard_map.145) | data formatting | bytes 262144

commit v3 on v2

--- a/solution.py
+++ b/solution.py
@@ -139,6 +139,8 @@
     back_in,
     gathered,
     weight,
+    halo,
+    gate,
     load_sem,
     send_sem,
     recv_sem,
@@ -152,6 +154,8 @@
     pair_recv,
     filt_send,
     filt_recv,
+    halo_send,
+    halo_recv,
 ):
     me = lax.axis_index("ctx")
     group = lax.axis_index("ch")
@@ -217,7 +221,7 @@
     loads[0].wait()
     flip = eye(tok, BF16)
     for h in range(2):
-        for s in range(3):
+        for s in range(2):
             block = streams[s, :, h * wide_half : (h + 1) * wide_half]
             turned = dot_nt(eye(wide_half, BF16), block)
             outgoing[h, :, s] = turned.reshape(n_ctx, 2, tok).astype(BF16)
@@ -238,6 +242,15 @@
             ).start()
 
         for_ctx_peers(send)
+
+    pltpu.make_async_remote_copy(
+        src_ref=streams.at[2, pl.ds(tok - 8, 8)],
+        dst_ref=halo,
+        send_sem=halo_send,
+        recv_sem=halo_recv,
+        device_id=(ctx_peer(1), group),
+        device_id_type=MESH,
+    ).start()
 
     depth, cols_out = weight.shape[2], weight.shape[3]
 
@@ -311,18 +324,20 @@
         for q in range(chunk // LANES):
             row = pl.multiple_of((i * (chunk // LANES) + q) * 8, 8)
             filt[half, pl.ds(row, 8), :] = value[:, q * LANES : (q + 1) * LANES]
-        part = filt.at[half, pl.ds(pl.multiple_of(i * (chunk // 16), chunk // 16), chunk // 16)]
+        return carry
+
+    count = seq_len // chunk
+    for part in range(2):
+        lax.fori_loop(part * count // 2, (part + 1) * count // 2, filter_step, 0)
+        done = filt.at[half, pl.ds(part * n_ctx * 4, n_ctx * 4)]
         pltpu.make_async_remote_copy(
-            src_ref=part,
-            dst_ref=part,
+            src_ref=done,
+            dst_ref=done,
             send_sem=filt_send,
             recv_sem=filt_recv,
             device_id=(partner, group),
             device_id_type=MESH,
         ).start()
-        return carry
-
-    lax.fori_loop(0, seq_len // chunk, filter_step, 0)
 
     tw_re, tw_im = twiddle[0], twiddle[1]
 
@@ -394,9 +409,10 @@
                 axis=1,
             )
             output = convolve(o, h, state) + direct * state
-            state = (shortened(h, o + 1) * output).astype(BF16).astype(F32)
+            if o == 0:
+                state = (shortened(h, 1) * output).astype(BF16).astype(F32)
         for c in range(2):
-            signal[h, 0, pl.ds(c, n_ctx, stride=2), :] = state[:, c * LANES : (c + 1) * LANES]
+            signal[h, 0, pl.ds(c, n_ctx, stride=2), :] = output[:, c * LANES : (c + 1) * LANES]
         back_out[h] = signal[h, 0].reshape(n_ctx, 2, tok).astype(BF16)
 
         pltpu.make_async_copy(back_out.at[h, me], back_in.at[h, me], back_recv.at[h]).start()
@@ -412,6 +428,15 @@
             ).start()
 
         for_ctx_peers(send_back)
+
+    pltpu.make_async_copy(halo, halo, halo_recv).wait()
+    near = streams[2].astype(F32)
+    ahead = jnp.where(me > 0, halo[...].astype(F32), 0.0)
+    at_row = lax.broadcasted_iota(jnp.int32, (tok, chl), 0)
+    one = jnp.where(at_row == 0, ahead[7:8], pltpu.roll(near, 1, 0))
+    two = jnp.where(at_row == 0, ahead[6:7], jnp.where(at_row == 1, ahead[7:8], pltpu.roll(near, 2, 0)))
+    made = short[2, 0:1] * near + short[2, 1:2] * one + short[2, 2:3] * two
+    gate[...] = made.astype(BF16).astype(F32)
 
     pltpu.make_async_copy(weight.at[:, half], weight.at[:, half], w_recv).wait()
     swap = pltpu.make_async_remote_copy(
@@ -427,7 +452,8 @@
     for h in range(2):
         pltpu.make_async_copy(back_in.at[h], back_in.at[h], back_recv.at[h]).wait()
         block = back_in[h].astype(F32).reshape(n_ctx * 2, tok)
-        gathered[h, group] = dot_nt(flip, block.astype(BF16)).astype(BF16)
+        turned = dot_nt(flip, block.astype(BF16))
+        gathered[h, group] = (gate[:, h * wide_half : (h + 1) * wide_half] * turned).astype(BF16)
         for d in range(1, n_ch):
             pltpu.make_async_remote_copy(
                 src_ref=gathered.at[h, group],
@@ -457,6 +483,7 @@
         pltpu.make_async_copy(sent, sent, back_send.at[h]).wait()
         sent = gathered.at[h, pl.ds(0, n_ch - 1)]
         pltpu.make_async_copy(sent, sent, ring_send.at[h]).wait()
+    pltpu.make_async_copy(halo, halo, halo_send).wait()
     sent = weight.at[pl.ds(0, n_ch - 1), half]
     pltpu.make_async_copy(sent, sent, w_send).wait()
 
@@ -506,21 +533,23 @@
         staged = [vmem(args[i]) for i in (0, 1, 2, 3, 4, 5, 6, 7, 8, 10, 11, 12, 13, 14)]
         dma = pltpu.SemaphoreType.DMA
         return pl.pallas_call(
-            functools.partial(kernel, n_ctx, n_ch, min(512, seq_len), sine_terms()),
-            out_shape=jax.ShapeDtypeStruct((tok, cols_out), BF16),
+            functools.partial(kernel, n_ctx, n_ch, min(1024, seq_len // 2), sine_terms()),
+            out_shape=pltpu.VMEM((tok, cols_out), BF16),
             in_specs=[pl.BlockSpec(memory_space=pl.ANY)] * len(args),
             out_specs=pl.BlockSpec(memory_space=pltpu.VMEM),
             scratch_shapes=staged
             + [
-                pltpu.VMEM((2, n_ctx, 3, 2, tok), BF16),
-                pltpu.VMEM((2, n_ctx, 3, 2, tok), BF16),
-                pltpu.VMEM((2, 3, n_ctx * 2, tok), F32),
+                pltpu.VMEM((2, n_ctx, 2, 2, tok), BF16),
+                pltpu.VMEM((2, n_ctx, 2, 2, tok), BF16),
+                pltpu.VMEM((2, 2, n_ctx * 2, tok), F32),
                 pltpu.VMEM((2, n_ctx * 8, LANES), F32),
                 pltpu.VMEM((2, 4 * kept, 2 * LANES), F32),
                 pltpu.VMEM((2, n_ctx, 2, tok), BF16),
                 pltpu.VMEM((2, n_ctx, 2, tok), BF16),
                 pltpu.VMEM((2, n_ch, tok, chl // 2), BF16),
                 pltpu.VMEM((n_ch, 2, chl // 2, cols_out), BF16),
+                pltpu.VMEM((8, chl), BF16),
+                pltpu.VMEM((tok, chl), F32),
                 dma((14,)),
                 dma((2,)),
                 dma((2,)),
@@ -528,6 +557,8 @@
                 dma((2,)),
                 dma((2,)),
                 dma((2, n_ch)),
+                dma,
+                dma,
                 dma,
                 dma,
                 dma,

time: 48.1 us -> 45.1 us (0.938)
  Pallas kernels: 46.3 us -> 44.3 us
  local copies, waits for them, and re-layouts: 1.57 us -> 0.66 us
    pallas_call x1, Pallas kernels: 46.3 us -> 44.3 us  [per_device(): pl.pallas_call(functools.partial(kernel, n_ctx, n_ch, min(1024, seq_len /...]
    unnamed x1, local copies, waits for them, and re-layouts: 1.57 us -> 0.66 us
where the time goes in v3:
time: 45.1 us; the launch traced here: 45 us
  Pallas kernels  44.3 us (98%)
  local copies, waits for them, and re-layouts  0.66 us (1%)
    pallas_call x1, Pallas kernels, per_device(): pl.pallas_call(functools.partial(kernel, n_ctx, n_ch, min(1024, seq_len /...  44.3 us

profile of v3, /device:TPU:1, one launch (start us, length us, event | category | flops | bytes accessed | tf_op | source)
XLA Modules:
  0.0 45.0 jit_solution(3214162016269697314)
XLA Ops:
  0.0 44.3 %shard_map.145 = bf16[128,512]{1,0:T(8,128)(2,1)S(1)} custom-call(bf16[3,128,256]{2,1,0:T(8,128)(2,1)} %streams_in.1, f32[3,3,256]{2,1,0:T(4,128)} %short_in.1, bf16[5,2,64]{2,1,0:T(2,128)(2,1)} %bitcast.1, f32[2,2,64]{2,1,0:T(2,128)} %bias_in.1, bf16[2,64,64]{2,1,0:T(8,128)(2,1)} %mid_in.1, f32[2,64]{1,0:T(2,128)} %freq_in.1, bf16[2,64,256]{2,1,0:T(8,128)(2,1)} %last_in.1, ...), custom_call_target="tpu_custom_call" | custom-call | tf_op jit(solution)/shard_map/pallas_call | solution.py:535
  44.3 0.7 %copy.17 = bf16[128,512]{1,0:T(8,128)(2,1)} copy(bf16[128,512]{1,0:T(8,128)(2,1)S(1)} %shard_map.145) | data formatting | bytes 262144

commit v4 on v3

v4 whole, which is shorter than its diff:
```python
import functools
import math

import jax
import jax.numpy as jnp
import numpy as np
from jax import lax
from jax.experimental import pallas as pl
from jax.experimental.pallas import tpu as pltpu
from jax.sharding import PartitionSpec as P

MESH = pl.DeviceIdType.MESH
BF16 = jnp.bfloat16
F32 = jnp.float32
EMB = 5
LANES = 128


def split_table(table):
    high = table.astype(np.float32).astype(jnp.bfloat16)
    low = (table - high.astype(np.float64)).astype(np.float32).astype(jnp.bfloat16)
    return np.stack([high, low])


def transform_tables(rows, kept):
    total = 2 * rows * LANES
    k = np.arange(kept)[:, None]
    live = k <= rows
    a = np.arange(rows)[None, :]
    b = np.arange(LANES)[None, :]
    angle = 2.0 * np.pi * ((k * a) % (2 * rows)) / (2 * rows)
    cos_a = np.where(live, np.cos(angle), 0.0)
    sin_a = np.where(live, np.sin(angle), 0.0)
    first = np.concatenate([cos_a, -sin_a], axis=0)
    weight = np.where((k == 0) | (k == rows), 1.0, 2.0) / total
    last = np.concatenate([(weight * cos_a).T, (-weight * sin_a).T], axis=1)
    turn = 2.0 * np.pi * ((k * b) % total) / total
    twiddle = np.stack([np.cos(turn), -np.sin(turn)]).astype(np.float32)
    j = np.arange(LANES)[:, None]
    phase = 2.0 * np.pi * ((j * b) % LANES) / LANES
    cos_b, sin_b = np.cos(phase), np.sin(phase)
    forward = np.block([[cos_b, -sin_b], [sin_b, cos_b]])
    wide = np.concatenate([split_table(forward), split_table(forward.T)])
    return split_table(first), split_table(last), twiddle, wide


def feature_table(seq_len):
    positions = np.arange(seq_len, dtype=np.int32)
    rows = [positions.astype(np.float32) / np.float32(seq_len)]
    cosines, sines = [], []
    for band in range((EMB - 1) // 2):
        wrapped = (band + 1) * positions % seq_len
        angle = np.float32(2.0 * math.pi / seq_len) * wrapped.astype(np.float32)
        cosines.append(np.cos(angle))
        sines.append(np.sin(angle))
    table = np.zeros((8, seq_len), np.float32)
    table[:EMB] = np.stack(rows + cosines + sines)
    table[EMB] = 1.0
    return np.concatenate([table] * 3).astype(jnp.bfloat16)


def sine_terms():
    e = 0.25 * np.cos(np.pi * (np.arange(400) + 0.5) / 800)
    basis = np.stack([e ** (2 * i + 1) for i in range(4)], axis=1)
    scale = 1.0 / np.maximum(np.abs(np.sin(2 * np.pi * e)), 1e-3)
    terms = np.linalg.lstsq(basis * scale[:, None], np.sin(2 * np.pi * e) * scale, rcond=None)[0]
    return [float(np.float32(t)) for t in terms]


def dot(a, b):
    return jnp.dot(a, b, preferred_element_type=F32)


def dot_nt(a, b):
    return lax.dot_general(a, b, (((1,), (1,)), ((), ())), preferred_element_type=F32)


def two_rows(a, b):
    both = dot(a, b)
    rows = a.shape[0] // 2
    return both[:rows] + both[rows:]


def halves(x):
    high = x.astype(BF16)
    return high, (x - high.astype(F32)).astype(BF16)


def eye(n, dtype):
    rows = lax.broadcasted_iota(jnp.int32, (n, n), 0)
    cols = lax.broadcasted_iota(jnp.int32, (n, n), 1)
    return (rows == cols).astype(F32).astype(dtype)


def terms(x, count):
    parts = []
    for _ in range(count):
        part = x.astype(BF16).astype(F32)
        parts.append(part)
        x = x - part
    return parts


def kernel(
    n_ctx,
    n_ch,
    chunk,
    sine,
    streams_in,
    short_in,
    first_in,
    bias_in,
    mid_in,
    freq_in,
    last_in,
    decay_in,
    skip_in,
    weight_in,
    lead_in,
    tail_in,
    twiddle_in,
    wide_in,
    feat_in,
    out_ref,
    streams,
    short,
    first,
    bias,
    mid,
    freq,
    last,
    decay,
    skip,
    lead,
    tail,
    twiddle,
    wide,
    feat,
    outgoing,
    incoming,
    signal,
    filt,
    spectrum,
    back_out,
    back_in,
    gathered,
    weight,
    halo,
    gate,
    load_sem,
    send_sem,
    recv_sem,
    back_send,
    back_recv,
    ring_send,
    ring_recv,
    w_send,
    w_recv,
    pair_send,
    pair_recv,
    filt_send,
    filt_recv,
    halo_send,
    halo_recv,
):
    me = lax.axis_index("ctx")
    group = lax.axis_index("ch")
    half = lax.rem(me, 2)
    partner = me + 1 - 2 * half
    tok, chl = streams.shape[1], streams.shape[2]
    wide_half = chl // 2
    kept = twiddle.shape[1]
    seq_len = feat.shape[1]

    def ctx_peer(d):
        return lax.rem(me + d, n_ctx)

    def ch_peer(d):
        return lax.rem(group + d, n_ch)

    n_y = n_ch // 2
    ring = [(dy, dx) for dy in range(n_y) for dx in range(2) if dy or dx]
    ring.sort(key=lambda p: min(p[0], n_y - p[0]) + 2 * p[1])

    def ring_peer(step):
        dy, dx = step
        return lax.rem(group // 2 + dy, n_y) * 2 + lax.rem(group + dx, 2)

    my_z = lax.rem(me, n_ctx // 2) // 2

    n_z = n_ctx // 4
    my_x = me // (2 * n_z)

    def device_at(x, z, core):
        return x * (2 * n_z) + 2 * z + core

    def block_at(x, z, core):
        return lax.rem(z + n_z // 4, n_z) * 4 + 2 * x + core

    mine = block_at(my_x, my_z, half)
    my_class = mine // (n_ctx // 2)

    def for_plane(z, act):
        act(1 - my_x, z, 1 - half)
        act(1 - my_x, z, half)
        act(my_x, z, 1 - half)

    def weight_peer(d):
        return (ctx_peer(n_ctx // 2) if d % 2 else me, ch_peer(d))

    def for_ctx_peers(act):
        quarter = n_ctx // 4
        act(ctx_peer(quarter))
        act(ctx_peer(3 * quarter))

        def step(e, carry):
            act(ctx_peer(quarter + e))
            act(ctx_peer(quarter - e))
            act(ctx_peer(3 * quarter + e))
            act(ctx_peer(3 * quarter - e))
            return carry

        lax.fori_loop(1, quarter, step, 0)
        act(ctx_peer(2 * quarter))

    loads = []
    pairs = (
        (streams_in, streams),
        (feat_in, feat),
        (first_in, first),
        (bias_in, bias),
        (mid_in, mid),
        (freq_in, freq),
        (last_in, last),
        (decay_in, decay),
        (lead_in, lead),
        (twiddle_in, twiddle),
        (wide_in, wide),
        (short_in, short),
        (skip_in, skip),
        (tail_in, tail),
    )
    for i, (src, dst) in enumerate(pairs):
        copy = pltpu.make_async_copy(src, dst, load_sem.at[i])
        copy.start()
        loads.append(copy)

    barrier = pltpu.get_barrier_semaphore()

    def greet_ctx(peer):
        pl.semaphore_signal(barrier, inc=1, device_id=(peer, group), device_id_type=MESH)

    for_ctx_peers(greet_ctx)
    for d in range(1, n_ch):
        pl.semaphore_signal(barrier, inc=1, device_id=(me, ch_peer(d)), device_id_type=MESH)
        if d % 2:
            pl.semaphore_signal(barrier, inc=1, device_id=weight_peer(d), device_id_type=MESH)

    loads[0].wait()
    flip = eye(tok, BF16)
    turner = eye(chl, BF16)
    for s in range(2):
        turned = dot_nt(turner, streams[s])
        outgoing[:, s] = turned.reshape(n_ctx, 4, tok).astype(BF16)

    lane = lax.broadcasted_iota(jnp.int32, (1, chl), 1)

    def picked(row, c):
        return jnp.sum(jnp.where(lane == 4 * mine + c, row, 0.0), axis=1, keepdims=True)

    def forward(parts):
        high = parts[0]
        part = two_rows(lead[...].reshape(4 * kept, n_ctx), high)
        if len(parts) > 1:
            part = part + dot(lead[0], parts[1])
        rows = []
        for c in range(high.shape[1] // LANES):
            re = part[:kept, c * LANES : (c + 1) * LANES]
            im = part[kept:, c * LANES : (c + 1) * LANES]
            rows.append(jnp.concatenate([re * twiddle[0] - im * twiddle[1], re * twiddle[1] + im * twiddle[0]], axis=1))
        high, low = halves(jnp.concatenate(rows, axis=0))
        return two_rows(jnp.concatenate([high, low], axis=0), wide[0]) + dot(high, wide[1])

    def inverse(spec):
        high, low = halves(spec)
        part = two_rows(jnp.concatenate([high, low], axis=0), wide[2]) + dot(high, wide[3])
        cols = []
        for c in range(spec.shape[0] // kept):
            re = part[c * kept : (c + 1) * kept, :LANES]
            im = part[c * kept : (c + 1) * kept, LANES:]
            cols.append(jnp.concatenate([re * twiddle[0] + im * twiddle[1], im * twiddle[0] - re * twiddle[1]], axis=0))
        high, low = halves(jnp.concatenate(cols, axis=1))
        return two_rows(tail[...].reshape(2 * n_ctx, 2 * kept), high) + dot(tail[0], low)

    def make_spectrum(o):
        cols = [filt[o, pl.ds(4 * half + c, n_ctx, stride=8), :] for c in range(4)]
        spectrum[o] = forward(halves(jnp.concatenate(cols, axis=1)))

    def pass_filter(part, parts):
        rows = n_ctx * 8 // parts
        done = filt.at[half, pl.ds(part * rows, rows)]
        pltpu.make_async_remote_copy(
            src_ref=done,
            dst_ref=done,
            send_sem=filt_send,
            recv_sem=filt_recv,
            device_id=(partner, group),
            device_id_type=MESH,
        ).start()

    def make_filter(pass_on):
        for copy in loads[1:]:
            copy.wait()
        pick_rows = lax.broadcasted_iota(jnp.int32, (8, chl), 0)
        pick_cols = lax.broadcasted_iota(jnp.int32, (8, chl), 1)
        pick = jnp.zeros((8, chl), F32)
        for r in range(8):
            here = (pick_rows == r) & (pick_cols == 4 * (mine - half) + r)
            pick = jnp.where(here, 1.0, pick)

        hidden = mid.shape[1]
        turns = freq[pl.ds(half, 1), :] * (1.0 / (2.0 * math.pi))
        both = first[...].astype(F32)
        base = jnp.where(half == 0, both[:, 0, :], both[:, 1, :]) * turns
        shifts = bias[half] * turns - 0.25
        base = jnp.concatenate([base, shifts[0:1], jnp.zeros((8 - EMB - 1, hidden), F32)], axis=0)
        flip_h = eye(hidden, BF16)
        lift = dot_nt(flip_h, jnp.concatenate(terms(base, 3), axis=0).astype(BF16)).astype(BF16)
        mixed = terms(mid[half].astype(F32) * turns, 2)
        mixed = mixed + terms(shifts[1:2], 3) + [jnp.zeros((13, hidden), F32)]
        mix = dot_nt(flip_h, jnp.concatenate(mixed, axis=0).astype(BF16)).astype(BF16)
        pull = dot_nt(pick.astype(BF16), last[half]).astype(BF16)
        rate_row = jnp.where(pick > 0.0, decay[pl.ds(half, 1), :], 0.0)
        rate = jnp.sum(rate_row, axis=1, keepdims=True)
        gain = jnp.sqrt(2.0 * rate)
        ones = (lax.broadcasted_iota(jnp.int32, (16, chunk), 0) < 3).astype(F32).astype(BF16)

        def sine_of(t):
            e = 0.25 - jnp.abs(t - jnp.round(t))
            e2 = e * e
            acc = sine[-1]
            for term in sine[-2::-1]:
                acc = acc * e2 + term
            return (acc * e).astype(BF16)

        def filter_step(i, carry):
            start = pl.multiple_of(i * chunk, chunk)
            act_one = sine_of(dot(lift, feat[:, pl.ds(start, chunk)]))
            act_two = sine_of(dot(mix, jnp.concatenate([act_one, act_one, ones], axis=0)))
            raw = dot(pull, act_two)
            lag = (lax.broadcasted_iota(jnp.int32, (8, chunk), 1) + start).astype(F32)
            value = raw * jnp.exp(-rate * lag) * gain
            for q in range(chunk // LANES):
                row = pl.multiple_of((i * (chunk // LANES) + q) * 8, 8)
                filt[half, pl.ds(row, 8), :] = value[:, q * LANES : (q + 1) * LANES]
            return carry

        count = seq_len // chunk
        for part in range(2):
            lax.fori_loop(part * count // 2, (part + 1) * count // 2, filter_step, 0)
            if pass_on:
                pass_filter(part, 2)
        make_spectrum(half)

    early = my_z < n_ctx // 8

    pl.when(early)(functools.partial(make_filter, False))

    pl.semaphore_wait(barrier, n_ctx + n_ch - 2 + n_ch // 2)

    pltpu.make_async_copy(outgoing.at[mine], incoming.at[me], recv_sem).start()

    def send(x, z, core):
        pltpu.make_async_remote_copy(
            src_ref=outgoing.at[block_at(x, z, core)],
            dst_ref=incoming.at[me],
            send_sem=send_sem,
            recv_sem=recv_sem,
            device_id=(device_at(x, z, core), group),
            device_id_type=MESH,
        ).start()

    def send_far(e, carry):
        for off in (n_z // 2 - e, n_z // 2 + e):
            z = lax.rem(my_z + off, n_z)
            for_plane(z, send)
            send(my_x, z, half)
        return carry

    opposite = lax.rem(my_z + n_z // 2, n_z)
    for_plane(opposite, send)
    send(my_x, opposite, half)
    lax.fori_loop(1, n_z // 2, send_far, 0)
    for_plane(my_z, send)

    pltpu.make_async_remote_copy(
        src_ref=streams.at[2, pl.ds(tok - 8, 8)],
        dst_ref=halo,
        send_sem=halo_send,
        recv_sem=halo_recv,
        device_id=(ctx_peer(1), group),
        device_id_type=MESH,
    ).start()

    depth, cols_out = weight.shape[2], weight.shape[3]

    def weight_block(g):
        return weight_in.at[
            pl.ds(pl.multiple_of(half * depth, depth), depth),
            pl.ds(pl.multiple_of(g * cols_out, cols_out), cols_out),
        ]

    pltpu.make_async_copy(weight_block(group), weight.at[group, half], w_recv).start()
    for d in range(1, n_ch):
        pltpu.make_async_remote_copy(
            src_ref=weight_block(ch_peer(d)),
            dst_ref=weight.at[group, half],
            send_sem=w_send,
            recv_sem=w_recv,
            device_id=weight_peer(d),
            device_id_type=MESH,
        ).start()

    pl.when(early)(functools.partial(pass_filter, 0, 1))
    pl.when(jnp.logical_not(early))(functools.partial(make_filter, True))

    sent = filt.at[half]
    pltpu.make_async_copy(sent, sent, filt_send).wait()
    came = filt.at[1 - half]
    pltpu.make_async_copy(came, came, filt_recv).wait()
    make_spectrum(1 - half)

    def convolve(o, state):
        spec = forward((state.astype(BF16),))
        re, im = spec[:, :LANES], spec[:, LANES:]
        f_re, f_im = spectrum[o, :, :LANES], spectrum[o, :, LANES:]
        return inverse(jnp.concatenate([re * f_re - im * f_im, re * f_im + im * f_re], axis=1))

    row0 = lax.broadcasted_iota(jnp.int32, (n_ctx, LANES), 0) == 0
    lane_at = lax.broadcasted_iota(jnp.int32, (n_ctx, LANES), 1)

    def delayed(x, by):
        near = pltpu.roll(x, by, 1)
        carried = jnp.where(row0, 0.0, pltpu.roll(near, 1, 0))
        return jnp.where(lane_at < by, carried, near)

    def shortened(s):
        signal[s] = incoming[:, s].astype(F32).reshape(n_ctx * 4, tok)
        cols = []
        for c in range(4):
            x = signal[s, pl.ds(c, n_ctx, stride=4), :]
            taps = [picked(short[s, i : i + 1, :], c) for i in range(3)]
            cols.append(taps[0] * x + taps[1] * delayed(x, 1) + taps[2] * delayed(x, 2))
        return jnp.concatenate(cols, axis=1).astype(BF16).astype(F32)

    pltpu.make_async_copy(incoming, incoming, recv_sem).wait()
    state = shortened(0)
    for o in range(2):
        direct = jnp.concatenate(
            [jnp.broadcast_to(picked(skip[o : o + 1, :], c), (1, LANES)) for c in range(4)], axis=1
        )
        output = convolve(o, state) + direct * state
        if o == 0:
            state = (shortened(1) * output).astype(BF16).astype(F32)
    for c in range(4):
        signal[0, pl.ds(c, n_ctx, stride=4), :] = output[:, c * LANES : (c + 1) * LANES]
    back_out[...] = signal[0].reshape(n_ctx, 4, tok).astype(BF16)

    landing = back_in.at[my_class, lax.rem(mine, n_ctx // 2)]
    pltpu.make_async_copy(back_out.at[me], landing, back_recv.at[my_class]).start()

    def send_back(x, z, core):
        place = device_at(x, z, core)
        pltpu.make_async_remote_copy(
            src_ref=back_out.at[place],
            dst_ref=landing,
            send_sem=back_send,
            recv_sem=back_recv.at[my_class],
            device_id=(place, group),
            device_id_type=MESH,
        ).start()

    def send_plane(z, carry):
        for_plane(z, send_back)

        @pl.when(z != my_z)
        def _():
            send_back(my_x, z, half)

        return carry

    lax.fori_loop(0, n_z, send_plane, 0)

    pltpu.make_async_copy(halo, halo, halo_recv).wait()
    near = streams[2].astype(F32)
    ahead = jnp.where(me > 0, halo[...].astype(F32), 0.0)
    at_row = lax.broadcasted_iota(jnp.int32, (tok, chl), 0)
    one = jnp.where(at_row == 0, ahead[7:8], pltpu.roll(near, 1, 0))
    two = jnp.where(at_row == 0, ahead[6:7], jnp.where(at_row == 1, ahead[7:8], pltpu.roll(near, 2, 0)))
    made = short[2, 0:1] * near + short[2, 1:2] * one + short[2, 2:3] * two
    gate[...] = made.astype(BF16).astype(F32)

    for h in range(2):
        pltpu.make_async_copy(back_in.at[h], back_in.at[h], back_recv.at[h]).wait()
        block = back_in[h].astype(F32).reshape(wide_half, tok)
        turned = dot_nt(flip, block.astype(BF16))
        gathered[h, group] = (gate[:, h * wide_half : (h + 1) * wide_half] * turned).astype(BF16)
        for hop in ring[::-1]:
            pltpu.make_async_remote_copy(
                src_ref=gathered.at[h, group],
                dst_ref=gathered.at[h, group],
                send_sem=ring_send.at[h],
                recv_sem=ring_recv.at[h, group],
                device_id=(me, ring_peer(hop)),
                device_id_type=MESH,
            ).start()
        if h == 0:
            pltpu.make_async_copy(weight.at[:, half], weight.at[:, half], w_recv).wait()
            swap = pltpu.make_async_remote_copy(
                src_ref=weight.at[:, half],
                dst_ref=weight.at[:, half],
                send_sem=pair_send,
                recv_sem=pair_recv,
                device_id=(partner, group),
                device_id_type=MESH,
            )
            swap.start()

    swap.wait()

    total = jnp.zeros((tok, cols_out), F32)
    for h in range(2):
        for hop in [(0, 0)] + ring:
            peer = ring_peer(hop)
            if hop != (0, 0):
                came = gathered.at[h, peer]
                pltpu.make_async_copy(came, came, ring_recv.at[h, peer]).wait()
            total = total + dot(gathered[h, peer], weight[peer, h])
    out_ref[...] = total.astype(BF16)

    sent = outgoing.at[pl.ds(0, n_ctx - 1)]
    pltpu.make_async_copy(sent, sent, send_sem).wait()
    sent = back_out.at[pl.ds(0, n_ctx - 1)]
    pltpu.make_async_copy(sent, sent, back_send).wait()
    for h in range(2):
        sent = gathered.at[h, pl.ds(0, n_ch - 1)]
        pltpu.make_async_copy(sent, sent, ring_send.at[h]).wait()
    pltpu.make_async_copy(halo, halo, halo_send).wait()
    sent = weight.at[pl.ds(0, n_ch - 1), half]
    pltpu.make_async_copy(sent, sent, w_send).wait()


def solution(mesh):
    n_ctx, n_ch = mesh.shape["ctx"], mesh.shape["ch"]

    def per_device(
        streams,
        short_weight,
        filt_first,
        filt_bias,
        filt_mid,
        filt_freq,
        filt_last,
        decay,
        skip,
        out_weight,
    ):
        tok, chl = streams.shape[1], streams.shape[2]
        seq_len = tok * n_ctx
        kept = (n_ctx + 1 + 7) // 8 * 8
        cols_out = out_weight.shape[1] // n_ch
        lead, tail, twiddle, wide = transform_tables(n_ctx, kept)
        feat = feature_table(seq_len)
        args = (
            streams,
            short_weight,
            jnp.transpose(filt_first, (1, 0, 2)),
            filt_bias,
            filt_mid,
            filt_freq,
            filt_last,
            decay,
            skip,
            out_weight,
            jnp.asarray(lead),
            jnp.asarray(tail),
            jnp.asarray(twiddle),
            jnp.asarray(wide),
            jnp.asarray(feat),
        )

        def vmem(x):
            return pltpu.VMEM(x.shape, x.dtype)

        staged = [vmem(args[i]) for i in (0, 1, 2, 3, 4, 5, 6, 7, 8, 10, 11, 12, 13, 14)]
        dma = pltpu.SemaphoreType.DMA
        return pl.pallas_call(
            functools.partial(kernel, n_ctx, n_ch, min(1024, seq_len // 2), sine_terms()),
            out_shape=pltpu.VMEM((tok, cols_out), BF16),
            in_specs=[pl.BlockSpec(memory_space=pl.ANY)] * len(args),
            out_specs=pl.BlockSpec(memory_space=pltpu.VMEM),
            scratch_shapes=staged
            + [
                pltpu.VMEM((n_ctx, 2, 4, tok), BF16),
                pltpu.VMEM((n_ctx, 2, 4, tok), BF16),
                pltpu.VMEM((2, n_ctx * 4, tok), F32),
                pltpu.VMEM((2, n_ctx * 8, LANES), F32),
                pltpu.VMEM((2, 4 * kept, 2 * LANES), F32),
                pltpu.VMEM((n_ctx, 4, tok), BF16),
                pltpu.VMEM((2, n_ctx // 2, 4, tok), BF16),
                pltpu.VMEM((2, n_ch, tok, chl // 2), BF16),
                pltpu.VMEM((n_ch, 2, chl // 2, cols_out), BF16),
                pltpu.VMEM((8, chl), BF16),
                pltpu.VMEM((tok, chl), F32),
                dma((14,)),
                dma,
                dma,
                dma,
                dma((2,)),
                dma((2,)),
                dma((2, n_ch)),
                dma,
                dma,
                dma,
                dma,
                dma,
                dma,
                dma,
                dma,
            ],
            compiler_params=pltpu.CompilerParams(collective_id=0, has_side_effects=True),
        )(*args)

    return jax.shard_map(
        per_device,
        mesh=mesh,
        in_specs=(
            P(None, "ctx", "ch"),
            P(None, None, "ch"),
            P(),
            P(),
            P(),
            P(),
            P(None, None, "ch"),
            P(None, "ch"),
            P(None, "ch"),
            P("ch", None),
        ),
        out_specs=P("ctx", "ch"),
        check_vma=False,
    )
```

time: 45.1 us -> 45 us (level)
  no operation moved by 1% of the time
where the time goes in v4:
time: 45 us; the launch traced here: 44.8 us
  Pallas kernels  44.2 us (98%)
  local copies, waits for them, and re-layouts  0.66 us (1%)
    pallas_call x1, Pallas kernels, per_device(): pl.pallas_call(functools.partial(kernel, n_ctx, n_ch, min(1024, seq_len /...  44.2 us

profile of v4, /device:TPU:1, one launch (start us, length us, event | category | flops | bytes accessed | tf_op | source)
XLA Modules:
  0.0 44.8 jit_solution(13571619054544691352)
XLA Ops:
  0.0 44.2 %shard_map.145 = bf16[128,512]{1,0:T(8,128)(2,1)S(1)} custom-call(bf16[3,128,256]{2,1,0:T(8,128)(2,1)} %streams_in.1, f32[3,3,256]{2,1,0:T(4,128)} %short_in.1, bf16[5,2,64]{2,1,0:T(2,128)(2,1)} %bitcast.1, f32[2,2,64]{2,1,0:T(2,128)} %bias_in.1, bf16[2,64,64]{2,1,0:T(8,128)(2,1)} %mid_in.1, f32[2,64]{1,0:T(2,128)} %freq_in.1, bf16[2,64,256]{2,1,0:T(8,128)(2,1)} %last_in.1, ...), custom_call_target="tpu_custom_call" | custom-call | tf_op jit(solution)/shard_map/pallas_call | solution.py:597
  44.2 0.7 %copy.17 = bf16[128,512]{1,0:T(8,128)(2,1)} copy(bf16[128,512]{1,0:T(8,128)(2,1)S(1)} %shard_map.145) | data formatting | bytes 262144

commit v5 on v4

--- a/solution.py
+++ b/solution.py
@@ -195,10 +195,14 @@
         return x * (2 * n_z) + 2 * z + core
 
     def block_at(x, z, core):
-        return lax.rem(z + n_z // 4, n_z) * 4 + 2 * x + core
+        far_side = z // (n_z // 2)
+        fold = z + far_side * (n_z - 1 - 2 * z)
+        return (2 * fold + far_side) * 4 + 2 * x + core
 
     mine = block_at(my_x, my_z, half)
-    my_class = mine // (n_ctx // 2)
+    n_class = back_in.shape[0]
+    class_rows = chl // n_class
+    my_class = mine // (n_ctx // n_class)
 
     def for_plane(z, act):
         act(1 - my_x, z, 1 - half)
@@ -466,7 +470,7 @@
         signal[0, pl.ds(c, n_ctx, stride=4), :] = output[:, c * LANES : (c + 1) * LANES]
     back_out[...] = signal[0].reshape(n_ctx, 4, tok).astype(BF16)
 
-    landing = back_in.at[my_class, lax.rem(mine, n_ctx // 2)]
+    landing = back_in.at[my_class, lax.rem(mine, n_ctx // n_class)]
     pltpu.make_async_copy(back_out.at[me], landing, back_recv.at[my_class]).start()
 
     def send_back(x, z, core):
@@ -498,17 +502,17 @@
     one = jnp.where(at_row == 0, ahead[7:8], pltpu.roll(near, 1, 0))
     two = jnp.where(at_row == 0, ahead[6:7], jnp.where(at_row == 1, ahead[7:8], pltpu.roll(near, 2, 0)))
     made = short[2, 0:1] * near + short[2, 1:2] * one + short[2, 2:3] * two
-    gate[...] = made.astype(BF16).astype(F32)
-
-    for h in range(2):
+    gate[...] = dot_nt(turner, made.astype(BF16))
+
+    for h in range(n_class):
         pltpu.make_async_copy(back_in.at[h], back_in.at[h], back_recv.at[h]).wait()
-        block = back_in[h].astype(F32).reshape(wide_half, tok)
-        turned = dot_nt(flip, block.astype(BF16))
-        gathered[h, group] = (gate[:, h * wide_half : (h + 1) * wide_half] * turned).astype(BF16)
+        block = back_in[h].astype(F32).reshape(class_rows, tok)
+        rows = slice(h * class_rows, (h + 1) * class_rows)
+        gathered[group, h] = (gate[rows, :] * block).astype(BF16)
         for hop in ring[::-1]:
             pltpu.make_async_remote_copy(
-                src_ref=gathered.at[h, group],
-                dst_ref=gathered.at[h, group],
+                src_ref=gathered.at[group, h],
+                dst_ref=gathered.at[group, h],
                 send_sem=ring_send.at[h],
                 recv_sem=ring_recv.at[h, group],
                 device_id=(me, ring_peer(hop)),
@@ -529,21 +533,24 @@
     swap.wait()
 
     total = jnp.zeros((tok, cols_out), F32)
-    for h in range(2):
+    per_half = n_class // 2
+    for p in range(2):
         for hop in [(0, 0)] + ring:
             peer = ring_peer(hop)
-            if hop != (0, 0):
-                came = gathered.at[h, peer]
-                pltpu.make_async_copy(came, came, ring_recv.at[h, peer]).wait()
-            total = total + dot(gathered[h, peer], weight[peer, h])
+            for h in range(p * per_half, (p + 1) * per_half):
+                if hop != (0, 0):
+                    came = gathered.at[peer, h]
+                    pltpu.make_async_copy(came, came, ring_recv.at[h, peer]).wait()
+            rows = gathered[peer, p * per_half : (p + 1) * per_half].reshape(wide_half, tok)
+            total = total + dot(dot_nt(flip, rows).astype(BF16), weight[peer, p])
     out_ref[...] = total.astype(BF16)
 
     sent = outgoing.at[pl.ds(0, n_ctx - 1)]
     pltpu.make_async_copy(sent, sent, send_sem).wait()
     sent = back_out.at[pl.ds(0, n_ctx - 1)]
     pltpu.make_async_copy(sent, sent, back_send).wait()
-    for h in range(2):
-        sent = gathered.at[h, pl.ds(0, n_ch - 1)]
+    for h in range(n_class):
+        sent = gathered.at[pl.ds(0, n_ch - 1), h]
         pltpu.make_async_copy(sent, sent, ring_send.at[h]).wait()
     pltpu.make_async_copy(halo, halo, halo_send).wait()
     sent = weight.at[pl.ds(0, n_ch - 1), half]
@@ -607,18 +614,18 @@
                 pltpu.VMEM((2, n_ctx * 8, LANES), F32),
                 pltpu.VMEM((2, 4 * kept, 2 * LANES), F32),
                 pltpu.VMEM((n_ctx, 4, tok), BF16),
-                pltpu.VMEM((2, n_ctx // 2, 4, tok), BF16),
-                pltpu.VMEM((2, n_ch, tok, chl // 2), BF16),
+                pltpu.VMEM((4, n_ctx // 4, 4, tok), BF16),
+                pltpu.VMEM((n_ch, 4, chl // 4, tok), BF16),
                 pltpu.VMEM((n_ch, 2, chl // 2, cols_out), BF16),
                 pltpu.VMEM((8, chl), BF16),
-                pltpu.VMEM((tok, chl), F32),
+                pltpu.VMEM((chl, tok), F32),
                 dma((14,)),
                 dma,
                 dma,
                 dma,
-                dma((2,)),
-                dma((2,)),
-                dma((2, n_ch)),
+                dma((4,)),
+                dma((4,)),
+                dma((4, n_ch)),
                 dma,
                 dma,
                 dma,

time: 45 us -> 44.3 us (0.984)
  Pallas kernels: 44.2 us -> 43.5 us
    pallas_call x1, Pallas kernels: 44.2 us -> 43.5 us  [per_device(): pl.pallas_call(functools.partial(kernel, n_ctx, n_ch, min(1024, seq_len /...]
where the time goes in v5:
time: 44.3 us; the launch traced here: 44.2 us
  Pallas kernels  43.5 us (98%)
  local copies, waits for them, and re-layouts  0.66 us (1%)
    pallas_call x1, Pallas kernels, per_device(): pl.pallas_call(functools.partial(kernel, n_ctx, n_ch, min(1024, seq_len /...  43.5 us

profile of v5, /device:TPU:1, one launch (start us, length us, event | category | flops | bytes accessed | tf_op | source)
XLA Modules:
  0.0 44.2 jit_solution(12277375029897076308)
XLA Ops:
  0.0 43.5 %shard_map.145 = bf16[128,512]{1,0:T(8,128)(2,1)S(1)} custom-call(bf16[3,128,256]{2,1,0:T(8,128)(2,1)} %streams_in.1, f32[3,3,256]{2,1,0:T(4,128)} %short_in.1, bf16[5,2,64]{2,1,0:T(2,128)(2,1)} %bitcast.1, f32[2,2,64]{2,1,0:T(2,128)} %bias_in.1, bf16[2,64,64]{2,1,0:T(8,128)(2,1)} %mid_in.1, f32[2,64]{1,0:T(2,128)} %freq_in.1, bf16[2,64,256]{2,1,0:T(8,128)(2,1)} %last_in.1, ...), custom_call_target="tpu_custom_call" | custom-call | tf_op jit(solution)/shard_map/pallas_call | solution.py:604
  43.5 0.7 %copy.17 = bf16[128,512]{1,0:T(8,128)(2,1)} copy(bf16[128,512]{1,0:T(8,128)(2,1)S(1)} %shard_map.145) | data formatting | bytes 262144

commit v6 on v5

--- a/solution.py
+++ b/solution.py
@@ -510,6 +510,8 @@
         rows = slice(h * class_rows, (h + 1) * class_rows)
         gathered[group, h] = (gate[rows, :] * block).astype(BF16)
         for hop in ring[::-1]:
+            if h < 2 and hop[1] and hop[0]:
+                continue
             pltpu.make_async_remote_copy(
                 src_ref=gathered.at[group, h],
                 dst_ref=gathered.at[group, h],
@@ -530,19 +532,32 @@
             )
             swap.start()
 
+    beside = ring_peer((0, 1))
+    for h in range(2):
+        came = gathered.at[beside, h]
+        pltpu.make_async_copy(came, came, ring_recv.at[h, beside]).wait()
+        for hop in ring[::-1]:
+            if hop[1] == 0:
+                pltpu.make_async_remote_copy(
+                    src_ref=gathered.at[beside, h],
+                    dst_ref=gathered.at[beside, h],
+                    send_sem=ring_send.at[h],
+                    recv_sem=ring_recv.at[h, beside],
+                    device_id=(me, ring_peer(hop)),
+                    device_id_type=MESH,
+                ).start()
+
     swap.wait()
 
     total = jnp.zeros((tok, cols_out), F32)
-    per_half = n_class // 2
-    for p in range(2):
-        for hop in [(0, 0)] + ring:
-            peer = ring_peer(hop)
-            for h in range(p * per_half, (p + 1) * per_half):
-                if hop != (0, 0):
-                    came = gathered.at[peer, h]
-                    pltpu.make_async_copy(came, came, ring_recv.at[h, peer]).wait()
-            rows = gathered[peer, p * per_half : (p + 1) * per_half].reshape(wide_half, tok)
-            total = total + dot(dot_nt(flip, rows).astype(BF16), weight[peer, p])
+    for hop in [(0, 0)] + ring:
+        peer = ring_peer(hop)
+        if hop != (0, 0):
+            for h in range(2 if hop == (0, 1) else 0, n_class):
+                came = gathered.at[peer, h]
+                pltpu.make_async_copy(came, came, ring_recv.at[h, peer]).wait()
+        rows = dot_nt(flip, gathered[peer].reshape(chl, tok)).astype(BF16)
+        total = total + dot(rows, weight[peer].reshape(chl, cols_out))
     out_ref[...] = total.astype(BF16)
 
     sent = outgoing.at[pl.ds(0, n_ctx - 1)]

time: 44.3 us -> 44.3 us (level)
  no operation moved by 1% of the time
where the time goes in v6:
time: 44.3 us; the launch traced here: 44.1 us
  Pallas kernels  43.5 us (98%)
  local copies, waits for them, and re-layouts  0.66 us (1%)
    pallas_call x1, Pallas kernels, per_device(): pl.pallas_call(functools.partial(kernel, n_ctx, n_ch, min(1024, seq_len /...  43.5 us

profile of v6, /device:TPU:1, one launch (start us, length us, event | category | flops | bytes accessed | tf_op | source)
XLA Modules:
  0.0 44.1 jit_solution(14102030795126527083)
XLA Ops:
  0.0 43.5 %shard_map.145 = bf16[128,512]{1,0:T(8,128)(2,1)S(1)} custom-call(bf16[3,128,256]{2,1,0:T(8,128)(2,1)} %streams_in.1, f32[3,3,256]{2,1,0:T(4,128)} %short_in.1, bf16[5,2,64]{2,1,0:T(2,128)(2,1)} %bitcast.1, f32[2,2,64]{2,1,0:T(2,128)} %bias_in.1, bf16[2,64,64]{2,1,0:T(8,128)(2,1)} %mid_in.1, f32[2,64]{1,0:T(2,128)} %freq_in.1, bf16[2,64,256]{2,1,0:T(8,128)(2,1)} %last_in.1, ...), custom_call_target="tpu_custom_call" | custom-call | tf_op jit(solution)/shard_map/pallas_call | solution.py:619
  43.5 0.7 %copy.17 = bf16[128,512]{1,0:T(8,128)(2,1)} copy(bf16[128,512]{1,0:T(8,128)(2,1)S(1)} %shard_map.145) | data formatting | bytes 262144

commit v7 on v6

--- a/solution.py
+++ b/solution.py
@@ -408,6 +408,21 @@
 
     depth, cols_out = weight.shape[2], weight.shape[3]
 
+    pl.when(early)(functools.partial(pass_filter, 0, 1))
+    pl.when(jnp.logical_not(early))(functools.partial(make_filter, True))
+
+    sent = filt.at[half]
+    pltpu.make_async_copy(sent, sent, filt_send).wait()
+    came = filt.at[1 - half]
+    pltpu.make_async_copy(came, came, filt_recv).wait()
+    make_spectrum(1 - half)
+
+    def convolve(o, state):
+        spec = forward((state.astype(BF16),))
+        re, im = spec[:, :LANES], spec[:, LANES:]
+        f_re, f_im = spectrum[o, :, :LANES], spectrum[o, :, LANES:]
+        return inverse(jnp.concatenate([re * f_re - im * f_im, re * f_im + im * f_re], axis=1))
+
     def weight_block(g):
         return weight_in.at[
             pl.ds(pl.multiple_of(half * depth, depth), depth),
@@ -424,21 +439,6 @@
             device_id=weight_peer(d),
             device_id_type=MESH,
         ).start()
-
-    pl.when(early)(functools.partial(pass_filter, 0, 1))
-    pl.when(jnp.logical_not(early))(functools.partial(make_filter, True))
-
-    sent = filt.at[half]
-    pltpu.make_async_copy(sent, sent, filt_send).wait()
-    came = filt.at[1 - half]
-    pltpu.make_async_copy(came, came, filt_recv).wait()
-    make_spectrum(1 - half)
-
-    def convolve(o, state):
-        spec = forward((state.astype(BF16),))
-        re, im = spec[:, :LANES], spec[:, LANES:]
-        f_re, f_im = spectrum[o, :, :LANES], spectrum[o, :, LANES:]
-        return inverse(jnp.concatenate([re * f_re - im * f_im, re * f_im + im * f_re], axis=1))
 
     row0 = lax.broadcasted_iota(jnp.int32, (n_ctx, LANES), 0) == 0
     lane_at = lax.broadcasted_iota(jnp.int32, (n_ctx, LANES), 1)
@@ -510,8 +510,6 @@
         rows = slice(h * class_rows, (h + 1) * class_rows)
         gathered[group, h] = (gate[rows, :] * block).astype(BF16)
         for hop in ring[::-1]:
-            if h < 2 and hop[1] and hop[0]:
-                continue
             pltpu.make_async_remote_copy(
                 src_ref=gathered.at[group, h],
                 dst_ref=gathered.at[group, h],
@@ -520,32 +518,17 @@
                 device_id=(me, ring_peer(hop)),
                 device_id_type=MESH,
             ).start()
-        if h == 0:
-            pltpu.make_async_copy(weight.at[:, half], weight.at[:, half], w_recv).wait()
-            swap = pltpu.make_async_remote_copy(
-                src_ref=weight.at[:, half],
-                dst_ref=weight.at[:, half],
-                send_sem=pair_send,
-                recv_sem=pair_recv,
-                device_id=(partner, group),
-                device_id_type=MESH,
-            )
-            swap.start()
-
-    beside = ring_peer((0, 1))
-    for h in range(2):
-        came = gathered.at[beside, h]
-        pltpu.make_async_copy(came, came, ring_recv.at[h, beside]).wait()
-        for hop in ring[::-1]:
-            if hop[1] == 0:
-                pltpu.make_async_remote_copy(
-                    src_ref=gathered.at[beside, h],
-                    dst_ref=gathered.at[beside, h],
-                    send_sem=ring_send.at[h],
-                    recv_sem=ring_recv.at[h, beside],
-                    device_id=(me, ring_peer(hop)),
-                    device_id_type=MESH,
-                ).start()
+
+    pltpu.make_async_copy(weight.at[:, half], weight.at[:, half], w_recv).wait()
+    swap = pltpu.make_async_remote_copy(
+        src_ref=weight.at[:, half],
+        dst_ref=weight.at[:, half],
+        send_sem=pair_send,
+        recv_sem=pair_recv,
+        device_id=(partner, group),
+        device_id_type=MESH,
+    )
+    swap.start()
 
     swap.wait()
 
@@ -553,7 +536,7 @@
     for hop in [(0, 0)] + ring:
         peer = ring_peer(hop)
         if hop != (0, 0):
-            for h in range(2 if hop == (0, 1) else 0, n_class):
+            for h in range(n_class):
                 came = gathered.at[peer, h]
                 pltpu.make_async_copy(came, came, ring_recv.at[h, peer]).wait()
         rows = dot_nt(flip, gathered[peer].reshape(chl, tok)).astype(BF16)

time: 44.3 us -> 44.3 us (level)
  no operation moved by 1% of the time
where the time goes in v7:
time: 44.3 us; the launch traced here: 44.1 us
  Pallas kernels  43.5 us (98%)
  local copies, waits for them, and re-layouts  0.66 us (1%)
    pallas_call x1, Pallas kernels, per_device(): pl.pallas_call(functools.partial(kernel, n_ctx, n_ch, min(1024, seq_len /...  43.5 us

profile of v7, /device:TPU:1, one launch (start us, length us, event | category | flops | bytes accessed | tf_op | source)
XLA Modules:
  0.0 44.1 jit_solution(1782775857131831249)
XLA Ops:
  0.0 43.5 %shard_map.145 = bf16[128,512]{1,0:T(8,128)(2,1)S(1)} custom-call(bf16[3,128,256]{2,1,0:T(8,128)(2,1)} %streams_in.1, f32[3,3,256]{2,1,0:T(4,128)} %short_in.1, bf16[5,2,64]{2,1,0:T(2,128)(2,1)} %bitcast.1, f32[2,2,64]{2,1,0:T(2,128)} %bias_in.1, bf16[2,64,64]{2,1,0:T(8,128)(2,1)} %mid_in.1, f32[2,64]{1,0:T(2,128)} %freq_in.1, bf16[2,64,256]{2,1,0:T(8,128)(2,1)} %last_in.1, ...), custom_call_target="tpu_custom_call" | custom-call | tf_op jit(solution)/shard_map/pallas_call | solution.py:602
  43.5 0.7 %copy.17 = bf16[128,512]{1,0:T(8,128)(2,1)} copy(bf16[128,512]{1,0:T(8,128)(2,1)S(1)} %shard_map.145) | data formatting | bytes 262144
